TPU v7x, 512 devices: a whole 4x4x16 slice. The times are simulated.
512 devices in a mesh: feeder: 32 (over x, y, core), scen: 16 (over z).
Axes of the slice: x: 4, y: 4, z: 16, core: 2. Of those that a mesh axis runs over, the one named last changes fastest.
Arguments:
- anchor: bfloat16 [256, 24, 16384], P('scen', None, 'feeder'), may hold values from -6 to 6
- cost_lin: bfloat16 [256, 24, 16384], P('scen', None, 'feeder'), may hold values from -6 to 6
- dual: float32 [256, 24, 16384], P('scen', None, 'feeder'), may hold values from -4 to 4
- target: float32 [256, 24], P('scen'), may hold values from -4 to 4
- leaf_weight: float32 [256], P('scen'), may hold values from 1 to 10
- q_mat: bfloat16 [16384, 512], P('feeder'), may hold values from -0.25 to 0.25
- diag_gain: float32 [16384], P('feeder'), may hold values from 0.5 to 2
- block_mask: int32 [32, 4, 4], P('feeder'), may hold values from 0 to 1, as said below
- ancestor: int32 [24, 256], P(None, 'scen'), may hold values from 0 to 255, as said below
Outputs:
- setpoints: float32 [256, 24, 16384], P('scen', None, 'feeder')
- average: float32 [256, 24, 16384], P('scen', None, 'feeder')
- new_dual: float32 [256, 24, 16384], P('scen', None, 'feeder')
Inputs may be any that keep to these rules, and one draw needn't show every extreme that they name: `block_mask`: every diagonal block is present; the share of present off-diagonal blocks differs from feeder to feeder. ancestor[t, s] is the first leaf of the section-t tree node that holds leaf s: the leaves of a node are consecutive, ancestor[0, s] = 0, and every section-t node lies inside one section-(t-1) node. Nodes may span several groups at any section.
All inputs are finite; a program needn't handle non-finite values.
Results may differ from a plain program's by a relative error of at most 0.0003.
Values sent between devices are 32-bit elements; how exact they have to be, the bound alone decides.
No kernel may reach another device: no remote copies, remote signals or barrier semaphores. Data moves between devices by JAX's collectives and lax.ppermute only.
A program may use at most 64 MiB of HBM per device.

v0:
```python
import jax
import jax.numpy as jnp
from jax import lax
from jax.sharding import PartitionSpec as P

PROX_ITERS = 8


penalty = 1.0
step_size = 0.08
coupling = 4.0
power_limit = 2.0


def link_terms(earlier, later):
    return (
        later[0] + later[2][:, None] * earlier[0],
        later[1] + later[2] * earlier[1],
        earlier[2] * later[2],
    )


def local(anchor, cost_lin, dual, target, leaf_weight, q_mat, diag_gain, block_mask, ancestor):
    leaves, sections, nodes = anchor.shape
    rows = leaves * sections
    count = block_mask.shape[1]
    width = nodes // count
    total_nodes = lax.axis_size("feeder") * nodes
    start_pt = anchor.astype(jnp.float32)
    fixed_part = cost_lin.astype(jnp.float32) + dual - penalty * start_pt
    diag_term = 2.0 * diag_gain + penalty
    expand = jnp.repeat(jnp.repeat(block_mask[0], width, axis=0), width, axis=1).astype(
        jnp.bfloat16
    )
    q_eff = q_mat * expand
    state = start_pt
    for sweep in range(PROX_ITERS):
        flat = state.reshape(rows, nodes).astype(jnp.bfloat16)
        image = jnp.dot(flat, q_eff, preferred_element_type=jnp.float32)
        head = lax.psum(jnp.sum(state, axis=2), "feeder") / total_nodes
        grad = image.reshape(leaves, sections, nodes) + diag_term * state + fixed_part
        grad = grad + coupling * (head - target)[:, :, None]
        state = jnp.clip(state - step_size * grad, -power_limit, power_limit)
    highest = lax.Precision.HIGHEST
    weighted = leaf_weight[:, None, None] * state
    first_leaf = lax.axis_index("scen") * leaves
    local_id = jnp.maximum(ancestor - first_leaf, 0)
    slot_ids = jnp.arange(leaves, dtype=jnp.int32)
    member = (local_id[:, None, :] == slot_ids[None, :, None]).astype(jnp.float32)
    seg_sums = jnp.einsum("tgl,ltn->tgn", member, weighted, precision=highest)
    seg_weights = jnp.einsum("tgl,l->tg", member, leaf_weight, precision=highest)
    last_pick = (slot_ids[None, :] == local_id[:, leaves - 1][:, None]).astype(jnp.float32)
    first_pick = (slot_ids[None, :] == 0).astype(jnp.float32)
    tail_sum = jnp.einsum("tg,tgn->tn", last_pick, seg_sums, precision=highest)
    tail_weight = jnp.sum(last_pick * seg_weights, axis=1)
    continued = (ancestor[:, 0] < first_leaf).astype(jnp.float32)
    spanning = (ancestor[:, leaves - 1] < first_leaf).astype(jnp.float32)
    head_sum = seg_sums[:, 0, :] * continued[:, None]
    head_weight = seg_weights[:, 0] * continued
    gathered = (
        lax.all_gather(tail_sum[None], "scen", axis=0, tiled=True),
        lax.all_gather(tail_weight[None], "scen", axis=0, tiled=True),
        lax.all_gather(head_sum[None], "scen", axis=0, tiled=True),
        lax.all_gather(head_weight[None], "scen", axis=0, tiled=True),
        lax.all_gather(spanning[None], "scen", axis=0, tiled=True),
    )
    position = lax.axis_index("scen")
    group_ids = jnp.arange(gathered[0].shape[0], dtype=jnp.int32)
    blank = (jnp.zeros_like(tail_sum), jnp.zeros_like(tail_weight), jnp.ones_like(spanning))

    def forward_step(carry, item):
        group, part_sum, part_weight, part_flag = item
        joined = link_terms(carry, (part_sum, part_weight, part_flag))
        keep = group < position
        return (
            jax.tree.map(lambda new_val, old_val: jnp.where(keep, new_val, old_val), joined, carry),
            None,
        )

    def backward_step(carry, item):
        group, part_sum, part_weight, part_flag = item
        joined = link_terms(carry, (part_sum, part_weight, part_flag))
        keep = group > position
        return (
            jax.tree.map(lambda new_val, old_val: jnp.where(keep, new_val, old_val), joined, carry),
            None,
        )

    before, unused = lax.scan(
        forward_step, blank, (group_ids, gathered[0], gathered[1], gathered[4])
    )
    after, unused = lax.scan(
        backward_step, blank, (group_ids, gathered[2], gathered[3], gathered[4]), reverse=True
    )
    open_front = first_pick * continued[:, None]
    seg_total = (
        seg_sums
        + open_front[:, :, None] * before[0][:, None, :]
        + last_pick[:, :, None] * after[0][:, None, :]
    )
    weight_total = seg_weights + open_front * before[1][:, None] + last_pick * after[1][:, None]
    leaf_sums = jnp.einsum("tgl,tgn->ltn", member, seg_total, precision=highest)
    leaf_weights = jnp.einsum("tgl,tg->lt", member, weight_total, precision=highest)
    average = leaf_sums / leaf_weights[:, :, None]
    new_dual = dual + penalty * (state - average)
    return (state, average, new_dual)


def solution(mesh):
    return jax.shard_map(
        local,
        mesh=mesh,
        in_specs=(
            P("scen", None, "feeder"),
            P("scen", None, "feeder"),
            P("scen", None, "feeder"),
            P("scen", None),
            P("scen"),
            P("feeder", None),
            P("feeder"),
            P("feeder", None, None),
            P(None, "scen"),
        ),
        out_specs=(P("scen", None, "feeder"), P("scen", None, "feeder"), P("scen", None, "feeder")),
        check_vma=False,
    )
```

profile of v0, /device:TPU:32, one launch (start us, length us, event | category | flops | bytes accessed | tf_op | source)
XLA Modules:
  0.0 681.2 jit_solution(15530600553333728089)
XLA Ops:
  0.6 0.7 convert_bitcast_fusion
  1.4 0.6 broadcast_in_dim.11
  2.1 0.9 copy-done
  3.0 0.4 fusion.100
  3.9 68.3 %psum.56 = f32[16,24]{1,0:T(8,128)S(1)} all-reduce(f32[16,24]{1,0:T(8,128)S(1)} %convert_reduce_fusion), channel_id=1, replica_groups=mesh['feeder'=32,'scen'=16] {'feeder'}, use_global_device_ids=true, to_apply=%region_1.0 | all-reduce | flops 384 | bytes 3072 | tf_op jit(solution)/shard_map/psum | solution.py:40
  72.2 1.4 fusion.74
  73.6 63.7 %psum.57 = f32[16,24]{1,0:T(8,128)S(1)} all-reduce(f32[16,24]{1,0:T(8,128)S(1)} %get-tuple-element.314), channel_id=1, replica_groups=mesh['feeder'=32,'scen'=16] {'feeder'}, use_global_device_ids=true, to_apply=%region_3.4 | all-reduce | flops 384 | bytes 3072 | tf_op jit(solution)/shard_map/psum | solution.py:40
  137.4 0.9 fusion.93
  138.2 63.7 %psum.58 = f32[16,24]{1,0:T(8,128)S(1)} all-reduce(f32[16,24]{1,0:T(8,128)S(1)} %get-tuple-element.320), channel_id=1, replica_groups=mesh['feeder'=32,'scen'=16] {'feeder'}, use_global_device_ids=true, to_apply=%region_5.6 | all-reduce | flops 384 | bytes 3072 | tf_op jit(solution)/shard_map/psum | solution.py:40
  201.9 0.6 fusion.94
  202.5 63.7 %psum.59 = f32[16,24]{1,0:T(8,128)S(1)} all-reduce(f32[16,24]{1,0:T(8,128)S(1)} %get-tuple-element.322), channel_id=1, replica_groups=mesh['feeder'=32,'scen'=16] {'feeder'}, use_global_device_ids=true, to_apply=%region_7.8 | all-reduce | flops 384 | bytes 3072 | tf_op jit(solution)/shard_map/psum | solution.py:40
  266.2 0.6 fusion.95
  266.8 63.7 %psum.60 = f32[16,24]{1,0:T(8,128)S(1)} all-reduce(f32[16,24]{1,0:T(8,128)S(1)} %get-tuple-element.324), channel_id=1, replica_groups=mesh['feeder'=32,'scen'=16] {'feeder'}, use_global_device_ids=true, to_apply=%region_9.10 | all-reduce | flops 384 | bytes 3072 | tf_op jit(solution)/shard_map/psum | solution.py:40
  330.5 0.6 fusion.96
  331.1 63.7 %psum.61 = f32[16,24]{1,0:T(8,128)S(1)} all-reduce(f32[16,24]{1,0:T(8,128)S(1)} %get-tuple-element.326), channel_id=1, replica_groups=mesh['feeder'=32,'scen'=16] {'feeder'}, use_global_device_ids=true, to_apply=%region_11.12 | all-reduce | flops 384 | bytes 3072 | tf_op jit(solution)/shard_map/psum | solution.py:40
  394.8 1.4 fusion.97
  396.1 63.7 %psum.62 = f32[16,24]{1,0:T(8,128)S(1)} all-reduce(f32[16,24]{1,0:T(8,128)S(1)} %get-tuple-element.328), channel_id=1, replica_groups=mesh['feeder'=32,'scen'=16] {'feeder'}, use_global_device_ids=true, to_apply=%region_13.14 | all-reduce | flops 384 | bytes 3072 | tf_op jit(solution)/shard_map/psum | solution.py:40
  459.8 2.0 fusion.98
  461.8 63.7 %psum.63 = f32[16,24]{1,0:T(8,128)S(1)} all-reduce(f32[16,24]{1,0:T(8,128)S(1)} %get-tuple-element.330), channel_id=1, replica_groups=mesh['feeder'=32,'scen'=16] {'feeder'}, use_global_device_ids=true, to_apply=%region_15.16 | all-reduce | flops 384 | bytes 3072 | tf_op jit(solution)/shard_map/psum | solution.py:40
  525.5 0.6 copy-done.8
  526.2 1.4 broadcast_multiply_fusion
  527.5 0.7 copy-done.6
  528.3 1.0 fusion.48
  529.5 0.4 fusion.99
  529.9 37.7 %all-gather = f32[384,512]{1,0:T(8,128)S(1)} all-gather(f32[24,512]{1,0:T(8,128)S(1)} %bitcast.122), channel_id=2, replica_groups=mesh['feeder'=32,'scen'=16] {'scen'}, dimensions={0}, use_global_device_ids=true | all-gather | bytes 835584 | tf_op jit(solution)/shard_map/all_gather | solution.py:61
  568.0 1.3 dynamic-slice
  570.3 30.1 %all-reduce.3 = (f32[384]{0:T(512)S(1)}, f32[384]{0:T(512)S(1)}, f32[384]{0:T(512)S(1)}) all-reduce(f32[384]{0:T(512)S(1)} %fusion.86, f32[384]{0:T(512)S(1)} %fusion.84, f32[384]{0:T(512)S(1)} %dynamic-update-slice.1), channel_id=3, replica_groups=mesh['feeder'=32,'scen'=16] {'scen'}, use_global_device_ids=true, to_apply=%add | all-reduce | flops 1152 | bytes 9216
  600.6 23.5 %while.30 = (s32[]{:T(128)}, f32[24,512]{1,0:T(8,128)S(1)}, f32[24]{0:T(128)S(1)}, s32[16]{0:T(128)S(1)}, s32[]{:T(128)}, /*index=5*/f32[16,24,512]{2,1,0:T(8,12...) while((s32[]{:T(128)}, f32[24,512]{1,0:T(8,128)S(1)}, ...), condition=%wide.region_18.19_spmd.clone, body=%wide.region_17.18_spmd.clone.sunk | while | flops 49252 | bytes 148175 | solution.py:89
  600.6 0.7 dynamic_slice.91
  602.1 0.7 dynamic_slice.91
  603.5 0.7 dynamic_slice.91
  605.0 0.7 dynamic_slice.91
  606.5 0.7 dynamic_slice.91
  607.9 0.7 dynamic_slice.91
  609.4 0.7 dynamic_slice.91
  610.9 0.7 dynamic_slice.91
  612.3 0.7 dynamic_slice.91
  613.8 0.7 dynamic_slice.91
  615.3 0.7 dynamic_slice.91
  616.7 0.7 dynamic_slice.91
  618.2 0.7 dynamic_slice.91
  619.7 0.7 dynamic_slice.91
  621.1 0.7 dynamic_slice.91
  622.6 0.7 dynamic_slice.91
  624.2 30.1 %all_gather.18 = f32[16,24,512]{2,1,0:T(8,128)S(1)} all-gather(f32[1,24,512]{2,1,0:T(8,128)S(1)} %copy.24), channel_id=1, replica_groups=mesh['feeder'=32,'scen'=16] {'scen'}, dimensions={0}, use_global_device_ids=true | all-gather | bytes 835584 | tf_op jit(solution)/shard_map/all_gather | solution.py:63
  654.4 23.5 %while.31 = (s32[]{:T(128)}, f32[24,512]{1,0:T(8,128)S(1)}, f32[24]{0:T(128)S(1)}, s32[16]{0:T(128)S(1)}, s32[]{:T(128)}, /*index=5*/f32[16,24,512]{2,1,0:T(8,12...) while((s32[]{:T(128)}, f32[24,512]{1,0:T(8,128)S(1)}, ...), condition=%wide.region_20.21_spmd.clone, body=%wide.region_19.20_spmd.clone.sunk | while | flops 49253 | bytes 148195 | solution.py:92
  654.4 0.7 dynamic_slice.94
  655.9 0.7 dynamic_slice.94
  657.4 0.7 dynamic_slice.94
  658.9 0.7 dynamic_slice.94
  660.3 0.7 dynamic_slice.94
  661.8 0.7 dynamic_slice.94
  663.3 0.7 dynamic_slice.94
  664.7 0.7 dynamic_slice.94
  666.2 0.7 dynamic_slice.94
  667.7 0.7 dynamic_slice.94
  669.1 0.7 dynamic_slice.94
  670.6 0.7 dynamic_slice.94
  672.1 0.7 dynamic_slice.94
  673.5 0.7 dynamic_slice.94
  675.0 0.7 dynamic_slice.94
  676.5 0.7 dynamic_slice.94
  678.2 0.7 fusion.50
  679.5 1.7 subtract_add_fusion
  (125 shorter events, 6.0 us)
Async XLA Ops:
  0.6 1.4 copy-start.4
  2.0 1.0 copy-start
  3.0 0.7 copy-start.7
  3.0 69.2 %copy-start.2 = (f32[16,24,512]{2,1,0:T(8,128)S(1)}, f32[16,24,512]{2,1,0:T(8,128)}, u32[]{:S(2)}) copy-start(f32[16,24,512]{2,1,0:T(8,128)} %param.15) | copy-start | bytes 2359300
  3.8 68.4 %copy-start.5 = (f32[16,24]{1,0:T(8,128)S(1)}, f32[16,24]{1,0:T(8,128)}, u32[]{:S(2)}) copy-start(f32[16,24]{1,0:T(8,128)} %param.16) | copy-start | bytes 4612
  525.5 0.7 copy-start.8
  527.5 0.7 copy-start.6
  678.2 1.1 copy-start.1
  678.2 1.4 copy-start.3
where the time goes:
time: 682 us; the launch traced here: 681 us
  blocking collectives  612 us (90%)
  local copies, waits for them, and re-layouts  27 us (4%)
  loops' own time  22.6 us (3%)
  matrix products  10.1 us (1%)
  other arithmetic  7.87 us (1%)
    psum x8, blocking collectives, local(): head = lax.psum(jnp.sum(state, axis=2), 'feeder') / total_nodes  514 us
    all_gather x1, blocking collectives, local(): lax.all_gather(tail_sum[None], 'scen', axis=0, tiled=True)  37.7 us
    all_gather x1, blocking collectives, local(): lax.all_gather(head_sum[None], 'scen', axis=0, tiled=True)  30.1 us
    unnamed x1, blocking collectives  30.1 us
    dynamic_slice x32, local copies, waits for them, and re-layouts, local(): lax.scan(forward_step, blank, (group_ids, gathered[0], gathered[1], gathe...  21.2 us

commit v1 on v0

v1 whole, which is shorter than its diff:
```python
import jax
import jax.numpy as jnp
from jax import lax
from jax.sharding import PartitionSpec as P

PROX_ITERS = 8


penalty = 1.0
step_size = 0.08
coupling = 4.0
power_limit = 2.0


def feeder_sum(part, feeders):
    spread = jnp.broadcast_to(part, (feeders,) + part.shape)
    return jnp.sum(lax.all_to_all(spread, "feeder", 0, 0), axis=0)


def local(anchor, cost_lin, dual, target, leaf_weight, q_mat, diag_gain, block_mask, ancestor):
    leaves, sections, nodes = anchor.shape
    rows = leaves * sections
    count = block_mask.shape[1]
    width = nodes // count
    feeders = lax.axis_size("feeder")
    groups = lax.axis_size("scen")
    total_nodes = feeders * nodes
    highest = lax.Precision.HIGHEST
    start_pt = anchor.astype(jnp.float32)
    fixed_part = cost_lin.astype(jnp.float32) + dual - penalty * start_pt
    diag_term = 2.0 * diag_gain + penalty
    expand = jnp.repeat(jnp.repeat(block_mask[0], width, axis=0), width, axis=1).astype(
        jnp.bfloat16
    )
    q_eff = q_mat * expand
    state = start_pt
    for sweep in range(PROX_ITERS):
        flat = state.reshape(rows, nodes).astype(jnp.bfloat16)
        image = jnp.dot(flat, q_eff, preferred_element_type=jnp.float32)
        part = jnp.sum(state, axis=2).reshape(rows // 128, 128)
        head = feeder_sum(part, feeders).reshape(leaves, sections) / total_nodes
        grad = image.reshape(leaves, sections, nodes) + diag_term * state + fixed_part
        grad = grad + coupling * (head - target)[:, :, None]
        state = jnp.clip(state - step_size * grad, -power_limit, power_limit)

    first_leaf = lax.axis_index("scen") * leaves
    same = (ancestor[:, :, None] == ancestor[:, None, :]).astype(jnp.float32)
    weighted = leaf_weight[:, None, None] * state
    own_sum = jnp.einsum("tlr,rtn->ltn", same, weighted, precision=highest)
    own_weight = jnp.einsum("tlr,r->lt", same, leaf_weight, precision=highest)
    continued = (ancestor[:, 0] < first_leaf).astype(jnp.float32)
    spanning = (ancestor[:, leaves - 1] < first_leaf).astype(jnp.float32)
    tail_sum, tail_weight = own_sum[leaves - 1], own_weight[leaves - 1]
    head_sum, head_weight = own_sum[0] * continued[:, None], own_weight[0] * continued

    node_blocks = nodes // 128
    section_blocks = groups // node_blocks
    per = sections // section_blocks

    def to_owner(sums):
        cut = sums.reshape(section_blocks, per, node_blocks, 128)
        return cut.transpose(0, 2, 1, 3).reshape(groups, per, 128)

    scalars = jnp.stack([tail_weight, head_weight, spanning], axis=0)
    scalars = scalars.reshape(3, section_blocks, per).transpose(1, 0, 2)
    scalars = jnp.pad(scalars, ((0, 0), (0, 0), (0, 128 - per)))
    scalars = jnp.repeat(scalars, node_blocks, axis=0)
    sent = jnp.concatenate([to_owner(tail_sum), to_owner(head_sum), scalars], axis=1)
    got = lax.all_to_all(sent, "scen", 0, 0)
    tails, heads = got[:, :per], got[:, per : 2 * per]
    tail_w, head_w, span = (got[:, 2 * per + i, :per] for i in range(3))

    ids = jnp.arange(groups)
    between = (ids[None, None, :] > ids[:, None, None]) & (ids[None, None, :] < ids[None, :, None])
    broken = jnp.any(between[:, :, :, None] & (span[None, None, :, :] < 0.5), axis=2)
    upper = (ids[:, None] < ids[None, :])[:, :, None]
    link = jnp.where(upper & ~broken, 1.0, 0.0)
    before = jnp.sum(link[:, :, :, None] * tails[:, None], axis=0)
    after = jnp.sum(link[:, :, :, None] * heads[None, :], axis=1)
    before_w = jnp.sum(link * tail_w[:, None], axis=0)
    after_w = jnp.sum(link * head_w[None, :], axis=1)
    first_w = before_w + head_w + span * after_w
    last_w = tail_w + after_w + span * before_w
    span_n = span[:, :, None]
    first_avg = (before + heads + span_n * after) / first_w[:, :, None]
    last_avg = (tails + after + span_n * before) / last_w[:, :, None]
    back = lax.all_to_all(jnp.concatenate([first_avg, last_avg], axis=1), "scen", 0, 0)

    def from_owner(chunk):
        cut = chunk.reshape(section_blocks, node_blocks, per, 128)
        return cut.transpose(0, 2, 1, 3).reshape(sections, nodes)

    first_avg, last_avg = from_owner(back[:, :per]), from_owner(back[:, per:])
    in_last = (ancestor == ancestor[:, leaves - 1 :]).T[:, :, None]
    in_front = (ancestor < first_leaf).T[:, :, None]
    average = own_sum / own_weight[:, :, None]
    average = jnp.where(in_last, last_avg[None], jnp.where(in_front, first_avg[None], average))
    new_dual = dual + penalty * (state - average)
    return (state, average, new_dual)


def solution(mesh):
    return jax.shard_map(
        local,
        mesh=mesh,
        in_specs=(
            P("scen", None, "feeder"),
            P("scen", None, "feeder"),
            P("scen", None, "feeder"),
            P("scen", None),
            P("scen"),
            P("feeder", None),
            P("feeder"),
            P("feeder", None, None),
            P(None, "scen"),
        ),
        out_specs=(P("scen", None, "feeder"), P("scen", None, "feeder"), P("scen", None, "feeder")),
    )
```

time: 682 us -> 167 us (0.24)
  blocking collectives: 612 us -> 21.7 us
  waiting for transfers between devices: 0 us -> 69.6 us
  starting transfers between devices: 0 us -> 46.9 us
  loops' own time: 22.6 us -> 0 us
  local copies, waits for them, and re-layouts: 27 us -> 10.7 us
    psum x8 -> x0, blocking collectives: 514 us -> none  [local(): head = lax.psum(jnp.sum(state, axis=2), 'feeder') / total_nodes]
    all_to_all x0 -> x8, waiting for transfers between devices: none -> 69.6 us  [the longest x6 41.3 us: feeder_sum(): return jnp.sum(lax.all_to_all(spread, 'feeder', 0, 0), axis=0)]
    all_gather x2 -> x0, blocking collectives: 67.8 us -> none  [the longest x1 37.7 us: local(): lax.all_gather(tail_sum[None], 'scen', axis=0, tiled=True)]
    all_to_all x0 -> x8, starting transfers between devices: none -> 46.9 us  [the longest x6 26.9 us: feeder_sum(): return jnp.sum(lax.all_to_all(spread, 'feeder', 0, 0), axis=0)]
    unnamed x1 -> x0, blocking collectives: 30.1 us -> none
    another operation x2 -> x0, loops' own time: 22.6 us -> none  [the longest x1 11.3 us: local(): lax.scan(backward_step, blank, (group_ids, gathered[2], gathered[3], gath...]
    all_to_all x0 -> x2, blocking collectives: none -> 21.7 us  [feeder_sum(): return jnp.sum(lax.all_to_all(spread, 'feeder', 0, 0), axis=0)]
    dynamic_slice x32 -> x0, local copies, waits for them, and re-layouts: 21.2 us -> none  [local(): lax.scan(forward_step, blank, (group_ids, gathered[0], gathered[1], gathe...]
  transfers between devices with their start and end apart: 0 -> 8, of which waited for: 0 -> 8; matrix products, arithmetic and copies ran while one was open for 0% -> 2% of each run, Pallas kernels for 0% -> 0%
where the time goes in v1:
time: 167 us; the launch traced here: 166 us
  waiting for transfers between devices  69.6 us (42%)
  starting transfers between devices  46.9 us (28%)
  blocking collectives  21.7 us (13%)
  local copies, waits for them, and re-layouts  10.7 us (6%)
  matrix products  8.75 us (5%)
  other arithmetic  7.36 us (4%)
    all_to_all x6, waiting for transfers between devices, feeder_sum(): return jnp.sum(lax.all_to_all(spread, 'feeder', 0, 0), axis=0)  41.3 us
    all_to_all x6, starting transfers between devices, feeder_sum(): return jnp.sum(lax.all_to_all(spread, 'feeder', 0, 0), axis=0)  26.9 us
    all_to_all x2, blocking collectives, feeder_sum(): return jnp.sum(lax.all_to_all(spread, 'feeder', 0, 0), axis=0)  21.7 us
    all_to_all x1, starting transfers between devices, local(): got = lax.all_to_all(sent, 'scen', 0, 0)  15.2 us
    all_to_all x1, waiting for transfers between devices, local(): lax.all_to_all(jnp.concatenate([first_avg, last_avg], axis=1), 'scen', 0, 0)  14.4 us
    all_to_all x1, waiting for transfers between devices, local(): got = lax.all_to_all(sent, 'scen', 0, 0)  13.9 us
    dot_general x8, matrix products, local(): image = jnp.dot(flat, q_eff, preferred_element_type=jnp.float32)  6.93 us
    all_to_all x1, starting transfers between devices, local(): lax.all_to_all(jnp.concatenate([first_avg, last_avg], axis=1), 'scen', 0, 0)  4.88 us
  transfers between devices with their start and end apart: 8, of which 8 were waited for; matrix products, arithmetic and copies ran while one was open for 2% of the time, Pallas kernels for 0%

profile of v1, /device:TPU:32, one launch (start us, length us, event | category | flops | bytes accessed | tf_op | source)
XLA Modules:
  0.0 166.3 jit_solution(16578640700894607046)
XLA Ops:
  0.6 1.1 convert_reduce_fusion
  1.8 0.1 reshape.256
  1.9 0.6 broadcast_in_dim.56
  2.5 7.3 %all-to-all-start = ((f32[32,3,128]{2,1,0:T(4,128)}), f32[32,3,128]{2,1,0:T(4,128)S(1)}, u32[]{:S(2)}, u32[]{:S(2)}) async-start(f32[32,3,128]{2,1,0:T(4,128)} %broadcast_in_dim.56), calls=%async_computation | async-start | bytes 131072 | tf_op jit(solution)/shard_map/all_to_all | solution.py:17
  9.9 0.6 broadcast_in_dim.55
  10.6 0.9 copy-done
  11.5 0.4 fusion.85
  11.9 0.3 copy-done.8
  12.2 5.2 %all-to-all-done = f32[32,3,128]{2,1,0:T(4,128)S(1)} async-done(((f32[32,3,128]{2,1,0:T(4,128)}), f32[32,3,128]{2,1,0:T(4,128)S(1)}, u32[]{:S(2)}, u32[]{:S(2)}) %all-to-all-start) | async-done | bytes 49184 | tf_op jit(solution)/shard_map/all_to_all | solution.py:17
  17.5 0.6 copy-done.5
  18.1 1.4 fusion.57
  19.5 0.1 reshape.257
  19.7 10.9 %all_to_all.50 = f32[32,3,128]{2,1,0:T(4,128)S(1)} all-to-all(f32[32,3,128]{2,1,0:T(4,128)S(1)} %broadcast_in_dim.57), channel_id=1, replica_groups=mesh['feeder'=32,'scen'=16] {'feeder'}, dimensions={0} | all-to-all | bytes 98304 | tf_op jit(solution)/shard_map/all_to_all | solution.py:17
  30.6 0.1 div.67
  30.7 1.7 %fusion.79 = (f32[16,24]{1,0:T(8,128)S(1)}, f32[16,24,512]{2,1,0:T(8,128)}) fusion(f32[16,24]{1,0:T(8,128)S(1)} %subtract_multiply_fusion.6, f32[16,24,512]{2,1,0:T(8,128)S(1)} %get-tuple-element.14, bf16[512,512]{1,0:T(8,128)(2,1)S(1)} %bitcast_multiply_fusion, f32[16,24]{1,0:T(8,128)S(1)} %subtract_multiply_fusion.7, f32[16,24,512]{2,1,0:T(8,128)S(1)} %bitcast.103, ...), kind=kOutput, calls=%fused_computation.140 | convolution fusion | flops 206241408 | bytes 3283456 | tf_op jit(solution)/shard_map/dot_general | solution.py:39
  32.5 10.9 %all_to_all.51 = f32[32,3,128]{2,1,0:T(4,128)S(1)} all-to-all(f32[32,3,128]{2,1,0:T(4,128)S(1)} %broadcast_in_dim.112), channel_id=1, replica_groups=mesh['feeder'=32,'scen'=16] {'feeder'}, dimensions={0} | all-to-all | bytes 98304 | tf_op jit(solution)/shard_map/all_to_all | solution.py:17
  43.4 0.1 div.69
  43.5 2.0 %fusion.80 = (f32[16,24]{1,0:T(8,128)S(1)}, f32[16,24,512]{2,1,0:T(8,128)S(1)}) fusion(f32[16,24,512]{2,1,0:T(8,128)} %get-tuple-element.32, f32[16,24]{1,0:T(8,128)S(1)} %subtract_multiply_fusion.5, f32[16,24,512]{2,1,0:T(8,128)S(1)} %get-tuple-element.14, f32[512]{0:T(512)S(1)} %multiply_add_fusion.1, bf16[512,512]{1,0:T(8,128)(2,1)S(1)} %bitcast_multiply_fusion), kind=kOutput, calls=%fused_computation.141 | convolution fusion | flops 203095680 | bytes 2888704 | tf_op jit(solution)/shard_map/dot_general | solution.py:39
  45.5 0.1 reshape.259
  45.6 0.6 broadcast_in_dim.113
  46.2 4.0 %all-to-all-start.3 = ((f32[32,3,128]{2,1,0:T(4,128)}), f32[32,3,128]{2,1,0:T(4,128)S(1)}, u32[]{:S(2)}, u32[]{:S(2)}) async-start(f32[32,3,128]{2,1,0:T(4,128)} %broadcast_in_dim.113), calls=%async_computation.3 | async-start | bytes 131072 | tf_op jit(solution)/shard_map/all_to_all | solution.py:17
  50.3 7.4 %all-to-all-done.3 = f32[32,3,128]{2,1,0:T(4,128)S(1)} async-done(((f32[32,3,128]{2,1,0:T(4,128)}), f32[32,3,128]{2,1,0:T(4,128)S(1)}, u32[]{:S(2)}, u32[]{:S(2)}) %all-to-all-start.3) | async-done | bytes 49184 | tf_op jit(solution)/shard_map/all_to_all | solution.py:17
  57.8 0.1 div.71
  57.9 0.6 fusion.81
  58.5 0.1 reshape.260
  58.6 0.6 broadcast_in_dim.114
  59.2 4.0 %all-to-all-start.4 = ((f32[32,3,128]{2,1,0:T(4,128)}), f32[32,3,128]{2,1,0:T(4,128)S(1)}, u32[]{:S(2)}, u32[]{:S(2)}) async-start(f32[32,3,128]{2,1,0:T(4,128)} %broadcast_in_dim.114), calls=%async_computation.4 | async-start | bytes 131072 | tf_op jit(solution)/shard_map/all_to_all | solution.py:17
  63.3 0.8 fusion.58
  64.2 6.6 %all-to-all-done.4 = f32[32,3,128]{2,1,0:T(4,128)S(1)} async-done(((f32[32,3,128]{2,1,0:T(4,128)}), f32[32,3,128]{2,1,0:T(4,128)S(1)}, u32[]{:S(2)}, u32[]{:S(2)}) %all-to-all-start.4) | async-done | bytes 49184 | tf_op jit(solution)/shard_map/all_to_all | solution.py:17
  70.8 0.1 div.73
  70.9 0.6 fusion.82
  71.5 0.1 reshape.261
  71.6 0.6 broadcast_in_dim.115
  72.3 3.9 %all-to-all-start.5 = ((f32[32,3,128]{2,1,0:T(4,128)}), f32[32,3,128]{2,1,0:T(4,128)S(1)}, u32[]{:S(2)}, u32[]{:S(2)}) async-start(f32[32,3,128]{2,1,0:T(4,128)} %broadcast_in_dim.115), calls=%async_computation.5 | async-start | bytes 131072 | tf_op jit(solution)/shard_map/all_to_all | solution.py:17
  76.2 7.5 %all-to-all-done.5 = f32[32,3,128]{2,1,0:T(4,128)S(1)} async-done(((f32[32,3,128]{2,1,0:T(4,128)}), f32[32,3,128]{2,1,0:T(4,128)S(1)}, u32[]{:S(2)}, u32[]{:S(2)}) %all-to-all-start.5) | async-done | bytes 49184 | tf_op jit(solution)/shard_map/all_to_all | solution.py:17
  83.7 0.1 div.75
  83.8 0.6 fusion.83
  84.4 0.1 reshape.262
  84.5 0.6 broadcast_in_dim.116
  85.1 3.9 %all-to-all-start.6 = ((f32[32,3,128]{2,1,0:T(4,128)}), f32[32,3,128]{2,1,0:T(4,128)S(1)}, u32[]{:S(2)}, u32[]{:S(2)}) async-start(f32[32,3,128]{2,1,0:T(4,128)} %broadcast_in_dim.116), calls=%async_computation.6 | async-start | bytes 131072 | tf_op jit(solution)/shard_map/all_to_all | solution.py:17
  89.3 7.3 %all-to-all-done.6 = f32[32,3,128]{2,1,0:T(4,128)S(1)} async-done(((f32[32,3,128]{2,1,0:T(4,128)}), f32[32,3,128]{2,1,0:T(4,128)S(1)}, u32[]{:S(2)}, u32[]{:S(2)}) %all-to-all-start.6) | async-done | bytes 49184 | tf_op jit(solution)/shard_map/all_to_all | solution.py:17
  96.6 0.1 div.77
  96.7 0.6 fusion.84
  97.3 0.1 reshape.263
  97.4 0.6 broadcast_in_dim.117
  98.0 3.9 %all-to-all-start.7 = ((f32[32,3,128]{2,1,0:T(4,128)}), f32[32,3,128]{2,1,0:T(4,128)S(1)}, u32[]{:S(2)}, u32[]{:S(2)}) async-start(f32[32,3,128]{2,1,0:T(4,128)} %broadcast_in_dim.117), calls=%async_computation.7 | async-start | bytes 131072 | tf_op jit(solution)/shard_map/all_to_all | solution.py:17
  102.0 0.1 copy.116
  102.1 7.3 %all-to-all-done.7 = f32[32,3,128]{2,1,0:T(4,128)S(1)} async-done(((f32[32,3,128]{2,1,0:T(4,128)}), f32[32,3,128]{2,1,0:T(4,128)S(1)}, u32[]{:S(2)}, u32[]{:S(2)}) %all-to-all-start.7) | async-done | bytes 49184 | tf_op jit(solution)/shard_map/all_to_all | solution.py:17
  109.5 0.1 div.79
  109.6 0.5 broadcast_multiply_fusion
  110.1 1.0 fusion.40
  111.1 0.5 copy.173
  111.6 0.1 copy_multiply_fusion
  111.8 0.7 copy.118
  112.5 15.2 %all-to-all-start.8 = ((f32[16,15,128]{2,1,0:T(8,128)}), f32[16,15,128]{2,1,0:T(8,128)S(1)}, u32[]{:S(2)}, u32[]{:S(2)}) async-start(f32[16,15,128]{2,1,0:T(8,128)} %copy.118), calls=%async_computation.8 | async-start | bytes 262144 | tf_op jit(solution)/shard_map/all_to_all | solution.py:69
  127.7 13.9 %all-to-all-done.8 = f32[16,15,128]{2,1,0:T(8,128)S(1)} async-done(((f32[16,15,128]{2,1,0:T(8,128)}), f32[16,15,128]{2,1,0:T(8,128)S(1)}, u32[]{:S(2)}, u32[]{:S(2)}) %all-to-all-start.8) | async-done | bytes 122912 | tf_op jit(solution)/shard_map/all_to_all | solution.py:69
  141.9 1.7 %and_reduce_fusion = pred[16,16,6]{1,2,0:T(8,128)(4,1)S(1)} fusion(pred[16,6]{0,1:T(8,128)(4,1)S(1)} %broadcast_compare_fusion, pred[16,16,16]{2,1,0:T(8,128)(4,1)S(1)} %broadcast_and_fusion), kind=kLoop, calls=%fused_computation.58 | loop fusion | flops 47616 | bytes 5728 | tf_op jit(solution)/shard_map/reduce_or | solution.py:75
  143.6 0.1 multiply_reduce_fusion.3
  143.9 0.3 multiply_reduce_fusion
  144.2 0.1 add_divide_fusion
  144.3 0.7 copy.130
  145.0 4.9 %all-to-all-start.9 = ((f32[16,12,128]{2,1,0:T(8,128)}), f32[16,12,128]{2,1,0:T(8,128)S(1)}, u32[]{:S(2)}, u32[]{:S(2)}) async-start(f32[16,12,128]{2,1,0:T(8,128)} %copy.130), calls=%async_computation.9 | async-start | bytes 262144 | tf_op jit(solution)/shard_map/all_to_all | solution.py:87
  149.9 14.4 %all-to-all-done.9 = f32[16,12,128]{2,1,0:T(8,128)S(1)} async-done(((f32[16,12,128]{2,1,0:T(8,128)}), f32[16,12,128]{2,1,0:T(8,128)S(1)}, u32[]{:S(2)}, u32[]{:S(2)}) %all-to-all-start.9) | async-done | bytes 98336 | tf_op jit(solution)/shard_map/all_to_all | solution.py:87
  164.5 1.8 %subtract_add_fusion = (f32[16,24,512]{2,1,0:T(8,128)}, f32[16,24,512]{2,1,0:T(8,128)}) fusion(f32[16,24,512]{2,1,0:T(8,128)S(1)} %copy-done.3, f32[16,24,512]{2,1,0:T(8,128)S(1)} %get-tuple-element.44, f32[16,24]{1,0:T(8,128)S(1)} %bitcast.119, f32[24,512,16]{1,2,0:T(8,128)S(1)} %fusion.40, f32[24,512]{1,0:T(8,128)S(1)} %bitcast.108, ...), kind=kLoop, calls=%fused_computation.54 | loop fusion | flops 983040 | bytes 4032768 | tf_op jit(solution)/shard_map/add | solution.py:98
  (87 shorter events, 1.9 us)
Async XLA Ops:
  0.6 9.2 %copy-start.7 = (s32[1,4,4]{2,1,0:T(4,128)S(1)}, s32[1,4,4]{2,1,0:T(4,128)}, u32[]{:S(2)}) copy-start(s32[1,4,4]{2,1,0:T(4,128)} %param.16) | copy-start | bytes 196
  1.8 8.7 %copy-start.4 = (bf16[512,512]{1,0:T(8,128)(2,1)S(1)}, bf16[512,512]{1,0:T(8,128)(2,1)}, u32[]{:S(2)}) copy-start(bf16[512,512]{1,0:T(8,128)(2,1)} %param.14) | copy-start | bytes 1572868
  2.5 14.9 %all-to-all-start = ((f32[32,3,128]{2,1,0:T(4,128)}), f32[32,3,128]{2,1,0:T(4,128)S(1)}, u32[]{:S(2)}, u32[]{:S(2)}) async-start(f32[32,3,128]{2,1,0:T(4,128)} %broadcast_in_dim.56), calls=%async_computation | async-start | bytes 131072 | tf_op jit(solution)/shard_map/all_to_all | solution.py:17
  10.5 1.0 copy-start
  11.5 0.7 copy-start.8
  11.5 6.6 %copy-start.2 = (f32[16,24,512]{2,1,0:T(8,128)S(1)}, f32[16,24,512]{2,1,0:T(8,128)}, u32[]{:S(2)}) copy-start(f32[16,24,512]{2,1,0:T(8,128)} %param.11) | copy-start | bytes 2359300
  17.4 0.7 copy-start.5
  46.2 4.0 %copy-start.6 = (s32[24,16]{0,1:T(8,128)S(1)}, s32[24,16]{0,1:T(8,128)}, u32[]{:S(2)}) copy-start(s32[24,16]{0,1:T(8,128)} %param.17) | copy-start | bytes 4612
  46.2 11.5 %all-to-all-start.3 = ((f32[32,3,128]{2,1,0:T(4,128)}), f32[32,3,128]{2,1,0:T(4,128)S(1)}, u32[]{:S(2)}, u32[]{:S(2)}) async-start(f32[32,3,128]{2,1,0:T(4,128)} %broadcast_in_dim.113), calls=%async_computation.3 | async-start | bytes 131072 | tf_op jit(solution)/shard_map/all_to_all | solution.py:17
  59.2 4.0 %copy-start.9 = (f32[16]{0:T(128)S(1)}, f32[16]{0:T(128)}, u32[]{:S(2)}) copy-start(f32[16]{0:T(128)} %param.13) | copy-start | bytes 196
  59.2 11.5 %all-to-all-start.4 = ((f32[32,3,128]{2,1,0:T(4,128)}), f32[32,3,128]{2,1,0:T(4,128)S(1)}, u32[]{:S(2)}, u32[]{:S(2)}) async-start(f32[32,3,128]{2,1,0:T(4,128)} %broadcast_in_dim.114), calls=%async_computation.4 | async-start | bytes 131072 | tf_op jit(solution)/shard_map/all_to_all | solution.py:17
  72.3 11.4 %all-to-all-start.5 = ((f32[32,3,128]{2,1,0:T(4,128)}), f32[32,3,128]{2,1,0:T(4,128)S(1)}, u32[]{:S(2)}, u32[]{:S(2)}) async-start(f32[32,3,128]{2,1,0:T(4,128)} %broadcast_in_dim.115), calls=%async_computation.5 | async-start | bytes 131072 | tf_op jit(solution)/shard_map/all_to_all | solution.py:17
  85.1 11.4 %all-to-all-start.6 = ((f32[32,3,128]{2,1,0:T(4,128)}), f32[32,3,128]{2,1,0:T(4,128)S(1)}, u32[]{:S(2)}, u32[]{:S(2)}) async-start(f32[32,3,128]{2,1,0:T(4,128)} %broadcast_in_dim.116), calls=%async_computation.6 | async-start | bytes 131072 | tf_op jit(solution)/shard_map/all_to_all | solution.py:17
  98.0 11.4 %all-to-all-start.7 = ((f32[32,3,128]{2,1,0:T(4,128)}), f32[32,3,128]{2,1,0:T(4,128)S(1)}, u32[]{:S(2)}, u32[]{:S(2)}) async-start(f32[32,3,128]{2,1,0:T(4,128)} %broadcast_in_dim.117), calls=%async_computation.7 | async-start | bytes 131072 | tf_op jit(solution)/shard_map/all_to_all | solution.py:17
  110.1 54.4 %copy-start.1 = (f32[16,24,512]{2,1,0:T(8,128)}, f32[16,24,512]{2,1,0:T(8,128)S(1)}, u32[]{:S(2)}) copy-start(f32[16,24,512]{2,1,0:T(8,128)S(1)} %get-tuple-element.44) | copy-start | bytes 2359300
  112.5 29.1 %all-to-all-start.8 = ((f32[16,15,128]{2,1,0:T(8,128)}), f32[16,15,128]{2,1,0:T(8,128)S(1)}, u32[]{:S(2)}, u32[]{:S(2)}) async-start(f32[16,15,128]{2,1,0:T(8,128)} %copy.118), calls=%async_computation.8 | async-start | bytes 262144 | tf_op jit(solution)/shard_map/all_to_all | solution.py:69
  144.3 20.2 %copy-start.3 = (f32[16,24,512]{2,1,0:T(8,128)S(1)}, f32[16,24,512]{2,1,0:T(8,128)}, u32[]{:S(2)}) copy-start(f32[16,24,512]{2,1,0:T(8,128)} %param.11) | copy-start | bytes 2359300
  145.0 19.4 %all-to-all-start.9 = ((f32[16,12,128]{2,1,0:T(8,128)}), f32[16,12,128]{2,1,0:T(8,128)S(1)}, u32[]{:S(2)}, u32[]{:S(2)}) async-start(f32[16,12,128]{2,1,0:T(8,128)} %copy.130), calls=%async_computation.9 | async-start | bytes 262144 | tf_op jit(solution)/shard_map/all_to_all | solution.py:87

commit v2 on v1

v2 whole, which is shorter than its diff:
```python
import jax
import jax.numpy as jnp
from jax import lax
from jax.experimental import pallas as pl
from jax.experimental.pallas import tpu as pltpu
from jax.sharding import PartitionSpec as P

PROX_ITERS = 8
LANES = 128


penalty = 1.0
step_size = 0.08
coupling = 4.0
power_limit = 2.0

VMEM = pl.BlockSpec(memory_space=pltpu.VMEM)
SMEM = pl.BlockSpec(memory_space=pltpu.SMEM)
HBM = pl.BlockSpec(memory_space=pl.ANY)
PARAMS = pltpu.CompilerParams(vmem_limit_bytes=12 * 1024 * 1024)


def row_sums(block):
    total = block[:, :LANES]
    for start in range(LANES, block.shape[1], LANES):
        total = total + block[:, start : start + LANES]
    return jnp.sum(total.T, axis=0, keepdims=True)


def sum_kernel(anchor_ref, sums_ref):
    for i in range(anchor_ref.shape[0] // LANES):
        block = anchor_ref[i * LANES : (i + 1) * LANES, :].astype(jnp.float32)
        sums_ref[i : i + 1, :] = row_sums(block)


def affine(x, image, gain, fixed):
    return x * gain - (fixed + step_size * image)


def prep_kernel(
    first_ref, weight_ref, mask_ref, anchor_ref, cost_ref, dual_ref, q_ref, diag_ref, anc_ref,
    q_out, fixed_out, z_out, gain_out, same_out, recip_out, pick_out, cont_out, scalar_out,
):
    nodes = q_ref.shape[0]
    count = mask_ref.shape[0]
    width = nodes // count
    for i in range(count):
        for j in range(count):
            rows, cols = slice(i * width, (i + 1) * width), slice(j * width, (j + 1) * width)
            keep = mask_ref[i, j].astype(jnp.float32).astype(jnp.bfloat16)
            q_out[rows, cols] = q_ref[rows, cols] * keep
    gain = 1.0 - step_size * (2.0 * diag_ref[...] + penalty)
    gain_out[...] = gain
    start_pt = anchor_ref[...].astype(jnp.float32)
    fixed = step_size * (cost_ref[...].astype(jnp.float32) + dual_ref[...] - penalty * start_pt)
    fixed_out[...] = fixed
    image = jnp.dot(anchor_ref[...], q_out[...], preferred_element_type=jnp.float32)
    z_out[...] = affine(start_pt, image, gain, fixed)

    leaves = weight_ref.shape[0]
    sections = anc_ref.shape[0] // leaves
    first_leaf = first_ref[0]
    anc = [anc_ref[i * sections : (i + 1) * sections, :] for i in range(leaves)]
    run = []
    for i in range(leaves):
        rows = slice(i * sections, (i + 1) * sections)
        weight = jnp.full(anc[0].shape, weight_ref[i], jnp.float32)
        if i == 0:
            same = jnp.zeros(anc[0].shape, jnp.float32)
            run.append(weight)
        else:
            same = jnp.where(anc[i] == anc[i - 1], 1.0, 0.0)
            run.append(weight + same * run[-1])
        same_out[rows, :] = same
    for i in reversed(range(leaves - 1)):
        run[i] = jnp.where(anc[i + 1] == anc[i], run[i + 1], run[i])
    for i in range(leaves):
        rows = slice(i * sections, (i + 1) * sections)
        recip_out[rows, :] = 1.0 / run[i]
        front = jnp.where(anc[i] < first_leaf, 1.0, 0.0)
        pick_out[rows, :] = jnp.where(anc[i] == anc[-1], 2.0, front)
    cont = jnp.where(anc[0] < first_leaf, 1.0, 0.0)
    span = jnp.where(anc[-1] < first_leaf, 1.0, 0.0)
    cont_out[...] = cont
    lane = lax.broadcasted_iota(jnp.int32, anc[0].shape, 1)
    scalar_out[...] = jnp.where(lane == 0, run[-1], jnp.where(lane == 1, run[0] * cont, span))


def clipped(total_nodes, got_ref, target_ref, z_ref, x_ref):
    parts = jnp.sum(got_ref[...], axis=0)
    shift = (step_size * coupling) * (parts * (1.0 / total_nodes) - target_ref[...])
    for i in range(z_ref.shape[0] // LANES):
        rows = slice(i * LANES, (i + 1) * LANES)
        tile = jnp.broadcast_to(shift[i : i + 1, :], (LANES, LANES)).T
        for start in range(0, z_ref.shape[1], LANES):
            cols = slice(start, start + LANES)
            x_ref[rows, cols] = jnp.clip(z_ref[rows, cols] - tile, -power_limit, power_limit)


def step_kernel(
    total_nodes, got_ref, target_ref, z_ref, q_ref, fixed_ref, gain_ref, sums_ref, z_out, x_ref
):
    clipped(total_nodes, got_ref, target_ref, z_ref, x_ref)
    for i in range(x_ref.shape[0] // LANES):
        sums_ref[i : i + 1, :] = row_sums(x_ref[i * LANES : (i + 1) * LANES, :])
    x = x_ref[...]
    image = jnp.dot(x.astype(jnp.bfloat16), q_ref[...], preferred_element_type=jnp.float32)
    z_out[...] = affine(x, image, gain_ref[...], fixed_ref[...])


def last_kernel(
    total_nodes, weight_ref, got_ref, target_ref, z_ref, same_ref, recip_ref, cont_ref, scalar_ref,
    x_ref, own_ref, sent_ref, tail_ref, head_ref,
):
    clipped(total_nodes, got_ref, target_ref, z_ref, x_ref)
    leaves = weight_ref.shape[0]
    sections = cont_ref.shape[0]
    nodes = x_ref.shape[1]
    owners = sent_ref.shape[0]
    node_blocks = nodes // LANES
    per = sections * node_blocks // owners
    for start in range(0, nodes, LANES):
        cols = slice(start, start + LANES)
        run = []
        for i in range(leaves):
            rows = slice(i * sections, (i + 1) * sections)
            term = weight_ref[i] * x_ref[rows, cols]
            run.append(term if i == 0 else term + same_ref[rows, :] * run[-1])
        total = run[-1]
        tail_ref[:, cols] = total
        for i in reversed(range(leaves)):
            rows = slice(i * sections, (i + 1) * sections)
            if i < leaves - 1:
                later = slice((i + 1) * sections, (i + 2) * sections)
                total = jnp.where(same_ref[later, :] > 0.5, total, run[i])
            own_ref[rows, cols] = total * recip_ref[rows, :]
        head_ref[:, cols] = total * cont_ref[...]
    zeros = jnp.zeros((8 - per, LANES), jnp.float32)
    for owner in range(owners):
        block, col = owner // node_blocks, owner % node_blocks
        rows, cols = slice(block * per, (block + 1) * per), slice(col * LANES, (col + 1) * LANES)
        sent_ref[owner, 0:per, :] = tail_ref[rows, cols]
        sent_ref[owner, per:8, :] = zeros
        sent_ref[owner, 8 : 8 + per, :] = head_ref[rows, cols]
        sent_ref[owner, 8 + per : 16, :] = zeros
        sent_ref[owner, 16 : 16 + per, :] = scalar_ref[rows, :]
        sent_ref[owner, 16 + per : 24, :] = zeros


def owner_kernel(got_ref, back_ref):
    groups = got_ref.shape[0]
    shape = (8, LANES)
    tails = [got_ref[g, 0:8, :] for g in range(groups)]
    heads = [got_ref[g, 8:16, :] for g in range(groups)]
    scalars = [got_ref[g, 16:24, :] for g in range(groups)]
    spans = [jnp.broadcast_to(s[:, 2:3], shape) for s in scalars]
    tail_w = [jnp.broadcast_to(s[:, 0:1], shape) for s in scalars]
    head_w = [jnp.broadcast_to(s[:, 1:2], shape) for s in scalars]
    zero = jnp.zeros(shape, jnp.float32)
    before, before_w, after, after_w = [zero], [zero], [zero], [zero]
    for g in range(groups - 1):
        before.append(tails[g] + spans[g] * before[-1])
        before_w.append(tail_w[g] + spans[g] * before_w[-1])
    for g in reversed(range(1, groups)):
        after.insert(0, heads[g] + spans[g] * after[0])
        after_w.insert(0, head_w[g] + spans[g] * after_w[0])
    for g in range(groups):
        first_w = before_w[g] + head_w[g] + spans[g] * after_w[g]
        last_w = tail_w[g] + after_w[g] + spans[g] * before_w[g]
        first_w = jnp.where(first_w > 0.0, first_w, 1.0)
        last_w = jnp.where(last_w > 0.0, last_w, 1.0)
        back_ref[g, 0:8, :] = (before[g] + heads[g] + spans[g] * after[g]) / first_w
        back_ref[g, 8:16, :] = (tails[g] + after[g] + spans[g] * before[g]) / last_w


def final_kernel(
    got_ref, own_ref, pick_ref, x_ref, dual_ref, average_hbm, new_dual_hbm,
    first_ref, last_ref, average_ref, new_dual_ref, sems,
):
    owners = got_ref.shape[0]
    sections, nodes = first_ref.shape
    node_blocks = nodes // LANES
    per = sections * node_blocks // owners
    for owner in range(owners):
        block, col = owner // node_blocks, owner % node_blocks
        rows, cols = slice(block * per, (block + 1) * per), slice(col * LANES, (col + 1) * LANES)
        first_ref[rows, cols] = got_ref[owner, 0:per, :]
        last_ref[rows, cols] = got_ref[owner, 8 : 8 + per, :]
    leaves = x_ref.shape[0] // sections
    chunks = sems.shape[1]
    each = leaves // chunks
    copies = []
    for chunk in range(chunks):
        for i in range(chunk * each, (chunk + 1) * each):
            rows = slice(i * sections, (i + 1) * sections)
            pick = pick_ref[rows, :]
            for start in range(0, nodes, LANES):
                cols = slice(start, start + LANES)
                ends = jnp.where(pick > 1.5, last_ref[:, cols], first_ref[:, cols])
                average = jnp.where(pick > 0.5, ends, own_ref[rows, cols])
                average_ref[rows, cols] = average
                new_dual_ref[rows, cols] = dual_ref[rows, cols] + penalty * (
                    x_ref[rows, cols] - average
                )
        part = pl.ds(chunk * each * sections, each * sections)
        for n, (src, dst) in enumerate(((average_ref, average_hbm), (new_dual_ref, new_dual_hbm))):
            copy = pltpu.make_async_copy(src.at[part, :], dst.at[part, :], sems.at[n, chunk])
            copy.start()
            copies.append(copy)
    for copy in copies:
        copy.wait()


def call(kernel, inputs, outputs, in_specs=None, out_specs=None, scratch=(), name=None):
    return pl.pallas_call(
        kernel,
        out_shape=outputs,
        in_specs=in_specs or [VMEM] * len(inputs),
        out_specs=out_specs or jax.tree.map(lambda _: VMEM, outputs),
        scratch_shapes=scratch,
        compiler_params=PARAMS,
        name=name,
    )(*inputs)


def shaped(shape, dtype=jnp.float32):
    return jax.ShapeDtypeStruct(shape, dtype)


def gather_parts(part):
    spread = jnp.broadcast_to(part, (lax.axis_size("feeder"),) + part.shape)
    return lax.all_to_all(spread, "feeder", 0, 0)


def local(anchor, cost_lin, dual, target, leaf_weight, q_mat, diag_gain, block_mask, ancestor):
    leaves, sections, nodes = anchor.shape
    rows = leaves * sections
    groups = lax.axis_size("scen")
    total_nodes = lax.axis_size("feeder") * nodes
    flat = lambda a: a.reshape(rows, nodes)
    sums_shape = shaped((rows // LANES, LANES))
    full, thin, slab = shaped((rows, nodes)), shaped((rows, LANES)), shaped((sections, LANES))

    sums = call(sum_kernel, (flat(anchor),), sums_shape, name="start_sums")
    got = gather_parts(sums)
    target_rows = target.reshape(rows // LANES, LANES)
    first_leaf = (lax.axis_index("scen") * leaves).astype(jnp.int32).reshape(1)
    anc = jnp.broadcast_to(ancestor.T.reshape(rows, 1), (rows, LANES))
    q_eff, fixed, z, gain, same, recip, pick, cont, scalars = call(
        prep_kernel,
        (first_leaf, leaf_weight, block_mask[0], flat(anchor), flat(cost_lin), flat(dual), q_mat,
         diag_gain.reshape(1, nodes), anc),
        (shaped((nodes, nodes), jnp.bfloat16), full, full, shaped((1, nodes)), thin, thin, thin,
         slab, slab),
        in_specs=[SMEM] * 3 + [VMEM] * 6,
        name="prep",
    )
    for sweep in range(PROX_ITERS - 1):
        sums, z = call(
            lambda *refs: step_kernel(total_nodes, *refs),
            (got, target_rows, z, q_eff, fixed, gain),
            (sums_shape, full),
            scratch=(pltpu.VMEM((rows, nodes), jnp.float32),),
            name="prox_step",
        )
        got = gather_parts(sums)
    x, own, sent = call(
        lambda *refs: last_kernel(total_nodes, *refs),
        (leaf_weight, got, target_rows, z, same, recip, cont, scalars),
        (full, full, shaped((groups, 24, LANES))),
        in_specs=[SMEM] + [VMEM] * 7,
        scratch=(pltpu.VMEM((sections, nodes), jnp.float32),) * 2,
        name="last_step",
    )
    got = lax.all_to_all(sent, "scen", 0, 0)
    back = call(owner_kernel, (got,), shaped((groups, 16, LANES)), name="owner_chain")
    got = lax.all_to_all(back, "scen", 0, 0)
    average, new_dual = call(
        final_kernel,
        (got, own, pick, x, flat(dual)),
        (full, full),
        out_specs=(HBM, HBM),
        scratch=(
            (pltpu.VMEM((sections, nodes), jnp.float32),) * 2
            + (pltpu.VMEM((rows, nodes), jnp.float32),) * 2
            + (pltpu.SemaphoreType.DMA((2, 4)),)
        ),
        name="finish",
    )
    whole = lambda a: a.reshape(leaves, sections, nodes)
    return (whole(x), whole(average), whole(new_dual))


def solution(mesh):
    return jax.shard_map(
        local,
        mesh=mesh,
        in_specs=(
            P("scen", None, "feeder"),
            P("scen", None, "feeder"),
            P("scen", None, "feeder"),
            P("scen", None),
            P("scen"),
            P("feeder", None),
            P("feeder"),
            P("feeder", None, None),
            P(None, "scen"),
        ),
        out_specs=(P("scen", None, "feeder"), P("scen", None, "feeder"), P("scen", None, "feeder")),
        check_vma=False,
    )
```

time: 167 us -> 156 us (0.934)
  blocking collectives: 21.7 us -> 131 us
  waiting for transfers between devices: 69.6 us -> 0.01 us
  starting transfers between devices: 46.9 us -> 7.32 us
  matrix products: 8.75 us -> 0 us
  Pallas kernels: 0 us -> 7.61 us
  other arithmetic: 7.36 us -> 0 us
  local copies, waits for them, and re-layouts: 10.7 us -> 8.26 us
    all_to_all x2 -> x9, blocking collectives: 21.7 us -> 131 us  [the longest x7 79.9 us: gather_parts(): return lax.all_to_all(spread, 'feeder', 0, 0)]
    all_to_all x8 -> x1, waiting for transfers between devices: 69.6 us -> 0.01 us  [gather_parts(): return lax.all_to_all(spread, 'feeder', 0, 0)]
    all_to_all x8 -> x1, starting transfers between devices: 46.9 us -> 7.32 us  [gather_parts(): return lax.all_to_all(spread, 'feeder', 0, 0)]
    dot_general x10 -> x0, matrix products: 8.75 us -> none  [the longest x8 6.93 us: local(): image = jnp.dot(flat, q_eff, preferred_element_type=jnp.float32)]
    pallas_call x0 -> x12, Pallas kernels: none -> 7.61 us  [call(): pl.pallas_call(kernel, out_shape=outputs, in_specs=in_specs or [VMEM] * l...]
    unnamed x28 -> x26, local copies, waits for them, and re-layouts: 2.27 us -> 5.86 us
    reduce_sum x12 -> x0, other arithmetic: 3.35 us -> none  [the longest x2 2.54 us: local(): part = jnp.sum(state, axis=2).reshape(rows // 128, 128)]
    broadcast_in_dim x11 -> x10, local copies, waits for them, and re-layouts: 4.52 us -> 1.61 us  [the longest x2 0.89 us: local(): anc = jnp.broadcast_to(ancestor.T.reshape(rows, 1), (rows, LANES))]
  transfers between devices with their start and end apart: 8 -> 1, of which waited for: 8 -> 0; matrix products, arithmetic and copies ran while one was open for 2% -> 1% of each run, Pallas kernels for 0% -> 1%
where the time goes in v2:
time: 156 us; the launch traced here: 155 us
  blocking collectives  131 us (84%)
  local copies, waits for them, and re-layouts  8.26 us (5%)
  Pallas kernels  7.61 us (5%)
  starting transfers between devices  7.32 us (5%)
    all_to_all x7, blocking collectives, gather_parts(): return lax.all_to_all(spread, 'feeder', 0, 0)  79.9 us
    all_to_all x1, blocking collectives, local(): got = lax.all_to_all(sent, 'scen', 0, 0)  31.3 us
    all_to_all x1, blocking collectives, local(): got = lax.all_to_all(back, 'scen', 0, 0)  19.5 us
    pallas_call x12, Pallas kernels, call(): pl.pallas_call(kernel, out_shape=outputs, in_specs=in_specs or [VMEM] * l...  7.61 us
    all_to_all x1, starting transfers between devices, gather_parts(): return lax.all_to_all(spread, 'feeder', 0, 0)  7.32 us
    unnamed x26, local copies, waits for them, and re-layouts  5.86 us
  transfers between devices with their start and end apart: 1, of which 0 were waited for; matrix products, arithmetic and copies ran while one was open for 1% of the time, Pallas kernels for 1%

profile of v2, /device:TPU:32, one launch (start us, length us, event | category | flops | bytes accessed | tf_op | source)
XLA Modules:
  0.0 154.8 jit_solution(16816295261193464345)
XLA Ops:
  0.6 0.0 copy-start
  0.6 0.0 copy-start.1
  0.7 1.1 copy-done.1
  1.7 0.1 start_sums.1
  1.9 0.6 broadcast_in_dim.31
  2.5 7.3 %all-to-all-start = ((f32[32,3,128]{2,1,0:T(4,128)}), f32[32,3,128]{2,1,0:T(4,128)S(1)}, u32[]{:S(2)}, u32[]{:S(2)}) async-start(f32[32,3,128]{2,1,0:T(4,128)} %broadcast_in_dim.31), calls=%async_computation | async-start | bytes 131072 | tf_op jit(solution)/shard_map/all_to_all | solution.py:232
  9.8 0.8 reshape.38.refs_1_.refs_2_
  10.6 0.8 broadcast_in_dim.32
  11.4 0.0 copy-start.10
  11.4 0.0 copy-start.11
  11.4 0.0 copy-start.12
  11.4 0.1 broadcast_in_dim.33.anc_ref
  11.6 0.0 copy-done
  11.6 0.5 copy-done.10
  12.1 0.0 copy-done.11
  12.1 0.0 copy-done.12
  12.1 0.0 copy-start.2
  12.1 1.0 copy-done.2
  13.1 0.0 copy-start.4
  13.1 1.0 copy-done.4
  14.1 0.0 copy-start.5
  14.1 1.0 copy-done.5
  15.1 1.1 prep.1
  16.3 0.0 copy-start.6
  16.3 0.6 copy-done.6
  16.9 0.0 copy-start.8
  16.9 0.6 copy-done.8
  17.5 0.0 all-to-all-done.refs_0_
  17.5 0.5 prox_step.7
  18.0 14.7 %all_to_all.50.refs_0_ = f32[32,3,128]{2,1,0:T(4,128)S(1)} all-to-all(f32[32,3,128]{2,1,0:T(4,128)S(1)} %broadcast_in_dim.34), channel_id=1, replica_groups=mesh['feeder'=32,'scen'=16] {'feeder'}, dimensions={0} | all-to-all | bytes 98304 | tf_op jit(solution)/shard_map/all_to_all | solution.py:232
  32.7 0.5 prox_step.8
  33.2 10.9 %all_to_all.51.refs_0_ = f32[32,3,128]{2,1,0:T(4,128)S(1)} all-to-all(f32[32,3,128]{2,1,0:T(4,128)S(1)} %broadcast_in_dim.35), channel_id=1, replica_groups=mesh['feeder'=32,'scen'=16] {'feeder'}, dimensions={0} | all-to-all | bytes 98304 | tf_op jit(solution)/shard_map/all_to_all | solution.py:232
  44.0 0.5 prox_step.9
  44.5 10.9 %all_to_all.52.refs_0_ = f32[32,3,128]{2,1,0:T(4,128)S(1)} all-to-all(f32[32,3,128]{2,1,0:T(4,128)S(1)} %broadcast_in_dim.36), channel_id=1, replica_groups=mesh['feeder'=32,'scen'=16] {'feeder'}, dimensions={0} | all-to-all | bytes 98304 | tf_op jit(solution)/shard_map/all_to_all | solution.py:232
  55.4 0.5 prox_step.10
  55.9 10.9 %all_to_all.53.refs_0_ = f32[32,3,128]{2,1,0:T(4,128)S(1)} all-to-all(f32[32,3,128]{2,1,0:T(4,128)S(1)} %broadcast_in_dim.37), channel_id=1, replica_groups=mesh['feeder'=32,'scen'=16] {'feeder'}, dimensions={0} | all-to-all | bytes 98304 | tf_op jit(solution)/shard_map/all_to_all | solution.py:232
  66.7 0.5 prox_step.11
  67.2 10.9 %all_to_all.54.refs_0_ = f32[32,3,128]{2,1,0:T(4,128)S(1)} all-to-all(f32[32,3,128]{2,1,0:T(4,128)S(1)} %broadcast_in_dim.38), channel_id=1, replica_groups=mesh['feeder'=32,'scen'=16] {'feeder'}, dimensions={0} | all-to-all | bytes 98304 | tf_op jit(solution)/shard_map/all_to_all | solution.py:232
  78.1 0.5 prox_step.12
  78.6 10.9 %all_to_all.55.refs_0_ = f32[32,3,128]{2,1,0:T(4,128)S(1)} all-to-all(f32[32,3,128]{2,1,0:T(4,128)S(1)} %broadcast_in_dim.39), channel_id=1, replica_groups=mesh['feeder'=32,'scen'=16] {'feeder'}, dimensions={0} | all-to-all | bytes 98304 | tf_op jit(solution)/shard_map/all_to_all | solution.py:232
  89.4 0.5 prox_step.13
  89.9 0.0 copy-start.7
  89.9 0.0 copy-start.9
  90.0 10.9 %all_to_all.56.refs_1_ = f32[32,3,128]{2,1,0:T(4,128)S(1)} all-to-all(f32[32,3,128]{2,1,0:T(4,128)S(1)} %broadcast_in_dim.40), channel_id=1, replica_groups=mesh['feeder'=32,'scen'=16] {'feeder'}, dimensions={0} | all-to-all | bytes 98304 | tf_op jit(solution)/shard_map/all_to_all | solution.py:232
  100.8 0.0 copy-done.7
  100.8 0.0 copy-done.9
  100.8 1.7 %last_step.1 = (f32[384,512]{1,0:T(8,128)}, f32[384,512]{1,0:T(8,128)S(1)}, f32[16,24,128]{2,1,0:T(8,128)S(1)}) custom-call(f32[16]{0:T(128)S(1)} %copy-done.12, f32[32,3,128]{2,1,0:T(4,128)S(1)} %all_to_all.56.refs_1_, f32[3,128]{1,0:T(4,128)S(1)} %reshape.38.refs_1_.refs_2_, f32[384,512]{1,0:T(8,128)S(1)} %get-tuple-element.48.refs_3_, ...), custom_call_target="tpu_custom_call" | custom-call | tf_op jit(solution)/shard_map/last_step/pallas_call | solution.py:215
  102.6 0.0 copy-start.3
  102.6 31.3 %all_to_all.57.got_ref = f32[16,24,128]{2,1,0:T(8,128)S(1)} all-to-all(f32[16,24,128]{2,1,0:T(8,128)S(1)} %get-tuple-element.54), channel_id=1, replica_groups=mesh['feeder'=32,'scen'=16] {'scen'}, dimensions={0} | all-to-all | bytes 393216 | tf_op jit(solution)/shard_map/all_to_all | solution.py:275
  133.9 0.1 owner_chain.1
  134.0 19.5 %all_to_all.58.got_ref = f32[16,16,128]{2,1,0:T(8,128)S(1)} all-to-all(f32[16,16,128]{2,1,0:T(8,128)S(1)} %owner_chain.1), channel_id=1, replica_groups=mesh['feeder'=32,'scen'=16] {'scen'}, dimensions={0} | all-to-all | bytes 262144 | tf_op jit(solution)/shard_map/all_to_all | solution.py:277
  153.5 0.0 copy-done.3
  153.5 1.3 finish.1
  (7 shorter events, 0.1 us)
Async XLA Ops:
  0.6 10.9 %copy-start = (f32[16,24,512]{2,1,0:T(8,128)S(1)}, f32[16,24,512]{2,1,0:T(8,128)}, u32[]{:S(2)}) copy-start(f32[16,24,512]{2,1,0:T(8,128)} %param.11) | copy-start | bytes 2359300
  0.6 1.1 copy-start.1
  2.5 15.0 %all-to-all-start = ((f32[32,3,128]{2,1,0:T(4,128)}), f32[32,3,128]{2,1,0:T(4,128)S(1)}, u32[]{:S(2)}, u32[]{:S(2)}) async-start(f32[32,3,128]{2,1,0:T(4,128)} %broadcast_in_dim.31), calls=%async_computation | async-start | bytes 131072 | tf_op jit(solution)/shard_map/all_to_all | solution.py:232
  11.4 0.7 copy-start.10
  11.4 0.7 copy-start.11
  11.4 0.7 copy-start.12
  12.1 1.0 copy-start.2
  13.1 1.0 copy-start.4
  14.1 1.0 copy-start.5
  16.3 0.6 copy-start.6
  16.9 0.6 copy-start.8
  89.9 10.9 %copy-start.7 = (f32[24,128]{1,0:T(8,128)S(1)}, f32[24,128]{1,0:T(8,128)}, u32[]{:S(2)}) copy-start(f32[24,128]{1,0:T(8,128)} %copy-done.6) | copy-start | bytes 36868
  89.9 10.9 %copy-start.9 = (f32[24,128]{1,0:T(8,128)S(1)}, f32[24,128]{1,0:T(8,128)}, u32[]{:S(2)}) copy-start(f32[24,128]{1,0:T(8,128)} %copy-done.8) | copy-start | bytes 36868
  102.6 50.9 %copy-start.3 = (f32[384,512]{1,0:T(8,128)S(1)}, f32[384,512]{1,0:T(8,128)}, u32[]{:S(2)}) copy-start(f32[384,512]{1,0:T(8,128)} %get-tuple-element.53.x_ref) | copy-start | bytes 2359300

commit v3 on v2

v3 whole, which is shorter than its diff:
```python
import jax
import jax.numpy as jnp
from jax import lax
from jax.experimental import pallas as pl
from jax.experimental.pallas import tpu as pltpu
from jax.sharding import PartitionSpec as P

PROX_ITERS = 8
LANES = 128


penalty = 1.0
step_size = 0.08
coupling = 4.0
power_limit = 2.0

VMEM = pl.BlockSpec(memory_space=pltpu.VMEM)
SMEM = pl.BlockSpec(memory_space=pltpu.SMEM)
HBM = pl.BlockSpec(memory_space=pltpu.HBM)
PARAMS = pltpu.CompilerParams(vmem_limit_bytes=12 * 1024 * 1024)


def row_sums(block):
    total = block[:, :LANES]
    for start in range(LANES, block.shape[1], LANES):
        total = total + block[:, start : start + LANES]
    return jnp.sum(total.T, axis=0, keepdims=True)


def sum_kernel(anchor_hbm, sums_ref, anchor_ref, sems):
    copies = []
    for i in range(anchor_ref.shape[0] // LANES):
        part = pl.ds(i * LANES, LANES)
        copies.append(
            pltpu.make_async_copy(anchor_hbm.at[part, :], anchor_ref.at[part, :], sems.at[i])
        )
        copies[i].start()
    for i in range(anchor_ref.shape[0] // LANES):
        copies[i].wait()
        block = anchor_ref[i * LANES : (i + 1) * LANES, :].astype(jnp.float32)
        sums_ref[i : i + 1, :] = row_sums(block)


def affine(x, image, gain, fixed):
    return x * gain - (fixed + step_size * image)


def column(row):
    n = row.shape[1]
    down = lax.broadcasted_iota(jnp.int32, (n, n), 0)
    across = lax.broadcasted_iota(jnp.int32, (n, n), 1)
    spread = jnp.broadcast_to(row, (n, n))
    return jnp.sum(jnp.where(down == across, spread, 0.0), axis=1, keepdims=True)


def prep_kernel(
    first_ref, weight_ref, mask_ref, target_ref, anc_ref, diag_ref,
    anchor_hbm, cost_hbm, dual_hbm, q_hbm,
    q_out, fixed_out, z_out, gain_out, dual_out, thin_out,
    anchor_ref, cost_ref, q_ref, sems,
):
    moves = ((q_hbm, q_ref), (anchor_hbm, anchor_ref), (cost_hbm, cost_ref), (dual_hbm, dual_out))
    copies = [pltpu.make_async_copy(src, dst, sems.at[i]) for i, (src, dst) in enumerate(moves)]
    for copy in copies:
        copy.start()
    leaves, sections = anc_ref.shape
    rows_all = leaves * sections
    thin = (sections, LANES)
    first_leaf = first_ref[0].astype(jnp.float32)
    owner_of = anc_ref[...].astype(jnp.float32)
    anc = [jnp.broadcast_to(column(owner_of[i : i + 1, :]), thin) for i in range(leaves)]
    run, same = [], []
    for i in range(leaves):
        weight = jnp.full(thin, weight_ref[i], jnp.float32)
        same.append(jnp.where(anc[i] == anc[i - 1], 1.0, 0.0) if i else jnp.zeros(thin, jnp.float32))
        run.append(weight + same[i] * run[-1] if i else weight)
    for i in reversed(range(leaves - 1)):
        run[i] = jnp.where(same[i + 1] > 0.5, run[i + 1], run[i])
    for i in range(leaves):
        start = i * sections
        front = jnp.where(anc[i] < first_leaf, 1.0, 0.0)
        thin_out[start : start + sections, :] = same[i]
        thin_out[rows_all + start : rows_all + start + sections, :] = 1.0 / run[i]
        thin_out[2 * rows_all + start : 2 * rows_all + start + sections, :] = jnp.where(
            anc[i] == anc[-1], 2.0, front
        )
    cont = jnp.where(anc[0] < first_leaf, 1.0, 0.0)
    span = jnp.where(anc[-1] < first_leaf, 1.0, 0.0)
    end = 3 * rows_all
    thin_out[end : end + sections, :] = cont
    blocks = 8
    per = sections // 4
    section = lax.broadcasted_iota(jnp.int32, thin, 0)
    lane = lax.broadcasted_iota(jnp.int32, thin, 1)
    for block in range(4):
        place = section - block * per
        inside = (place >= 0) & (place < per)
        line = jnp.where(inside & (lane == place), run[-1], 0.0)
        line = jnp.where(inside & (lane == place + 8), run[0] * cont, line)
        line = jnp.where(inside & (lane == place + 16), span, line)
        spot = end + sections + block
        thin_out[spot : spot + 1, :] = jnp.sum(line, axis=0, keepdims=True)
    thin_out[end + sections + 4 : end + sections + blocks, :] = jnp.zeros((4, LANES), jnp.float32)
    gain = 1.0 - step_size * (2.0 * diag_ref[...] + penalty)
    gain_out[...] = gain

    count = mask_ref.shape[0]
    width = q_ref.shape[0] // count
    copies[0].wait()
    for i in range(count):
        for j in range(count):
            rows, cols = slice(i * width, (i + 1) * width), slice(j * width, (j + 1) * width)
            keep = mask_ref[i, j].astype(jnp.float32).astype(jnp.bfloat16)
            q_out[rows, cols] = q_ref[rows, cols] * keep
    copies[1].wait()
    image = jnp.dot(anchor_ref[...], q_out[...], preferred_element_type=jnp.float32)
    z_out[...] = image
    copies[2].wait()
    copies[3].wait()
    for i in range(leaves):
        rows = slice(i * sections, (i + 1) * sections)
        pull = (step_size * coupling) * column(target_ref[i : i + 1, :])
        start_pt = anchor_ref[rows, :].astype(jnp.float32)
        linear = cost_ref[rows, :].astype(jnp.float32) + dual_out[rows, :] - penalty * start_pt
        fixed = step_size * linear - pull
        fixed_out[rows, :] = fixed
        z_out[rows, :] = affine(start_pt, z_out[rows, :], gain, fixed)


def clipped(total_nodes, got_ref, z_ref, x_ref):
    shift = jnp.sum(got_ref[...], axis=0) * (step_size * coupling / total_nodes)
    for i in range(z_ref.shape[0] // LANES):
        rows = slice(i * LANES, (i + 1) * LANES)
        tile = jnp.broadcast_to(shift[i : i + 1, :], (LANES, LANES)).T
        for start in range(0, z_ref.shape[1], LANES):
            cols = slice(start, start + LANES)
            x_ref[rows, cols] = jnp.clip(z_ref[rows, cols] - tile, -power_limit, power_limit)


def step_kernel(
    total_nodes, got_ref, z_ref, q_ref, fixed_ref, gain_ref, sums_ref, z_out, x_ref
):
    clipped(total_nodes, got_ref, z_ref, x_ref)
    for i in range(x_ref.shape[0] // LANES):
        sums_ref[i : i + 1, :] = row_sums(x_ref[i * LANES : (i + 1) * LANES, :])
    x = x_ref[...]
    image = jnp.dot(x.astype(jnp.bfloat16), q_ref[...], preferred_element_type=jnp.float32)
    z_out[...] = affine(x, image, gain_ref[...], fixed_ref[...])


def last_kernel(
    total_nodes, weight_ref, got_ref, z_ref, thin_ref,
    x_hbm, own_ref, sent_ref,
    x_ref, tail_ref, head_ref, sem,
):
    clipped(total_nodes, got_ref, z_ref, x_ref)
    copy = pltpu.make_async_copy(x_ref, x_hbm, sem)
    copy.start()
    leaves = weight_ref.shape[0]
    rows_all, nodes = x_ref.shape
    sections = rows_all // leaves
    owners = sent_ref.shape[0]
    node_blocks = nodes // LANES
    per = sections * node_blocks // owners
    end = 3 * rows_all
    for start in range(0, nodes, LANES):
        cols = slice(start, start + LANES)
        run = []
        for i in range(leaves):
            rows = slice(i * sections, (i + 1) * sections)
            term = weight_ref[i] * x_ref[rows, cols]
            run.append(term if i == 0 else term + thin_ref[rows, :] * run[-1])
        total = run[-1]
        tail_ref[:, cols] = total
        for i in reversed(range(leaves)):
            rows = slice(i * sections, (i + 1) * sections)
            if i < leaves - 1:
                later = slice((i + 1) * sections, (i + 2) * sections)
                total = jnp.where(thin_ref[later, :] > 0.5, total, run[i])
            recip = slice(rows_all + i * sections, rows_all + (i + 1) * sections)
            own_ref[rows, cols] = total * thin_ref[recip, :]
        head_ref[:, cols] = total * thin_ref[end : end + sections, :]
    zeros = jnp.zeros((8 - per, LANES), jnp.float32)
    for owner in range(owners):
        block, col = owner // node_blocks, owner % node_blocks
        rows, cols = slice(block * per, (block + 1) * per), slice(col * LANES, (col + 1) * LANES)
        spot = end + sections + block
        sent_ref[owner, 0:per, :] = tail_ref[rows, cols]
        sent_ref[owner, per:8, :] = zeros
        sent_ref[owner, per : per + 1, :] = thin_ref[spot : spot + 1, :]
        sent_ref[owner, 8 : 8 + per, :] = head_ref[rows, cols]
        sent_ref[owner, 8 + per : 16, :] = zeros
    copy.wait()


def owner_kernel(got_ref, back_ref):
    per = back_ref.shape[1] * back_ref.shape[2] // 2
    groups = got_ref.shape[0]
    shape = (8, LANES)
    tails = [got_ref[g, 0:8, :] for g in range(groups)]
    heads = [got_ref[g, 8:16, :] for g in range(groups)]
    down = lax.broadcasted_iota(jnp.int32, shape, 0)
    across = lax.broadcasted_iota(jnp.int32, shape, 1)

    def scalars(g, first):
        line = jnp.broadcast_to(got_ref[g, per : per + 1, :], shape)
        mine = jnp.where(across == down + first, line, 0.0)
        return jnp.broadcast_to(jnp.sum(mine, axis=1, keepdims=True), shape)

    tail_w = [scalars(g, 0) for g in range(groups)]
    head_w = [scalars(g, 8) for g in range(groups)]
    spans = [scalars(g, 16) for g in range(groups)]
    zero = jnp.zeros(shape, jnp.float32)
    before, before_w, after, after_w = [zero], [zero], [zero], [zero]
    for g in range(groups - 1):
        before.append(tails[g] + spans[g] * before[-1])
        before_w.append(tail_w[g] + spans[g] * before_w[-1])
    for g in reversed(range(1, groups)):
        after.insert(0, heads[g] + spans[g] * after[0])
        after_w.insert(0, head_w[g] + spans[g] * after_w[0])
    for g in range(groups):
        first_w = before_w[g] + head_w[g] + spans[g] * after_w[g]
        last_w = tail_w[g] + after_w[g] + spans[g] * before_w[g]
        first_w = jnp.where(first_w > 0.0, first_w, 1.0)
        last_w = jnp.where(last_w > 0.0, last_w, 1.0)
        first = (before[g] + heads[g] + spans[g] * after[g]) / first_w
        last = (tails[g] + after[g] + spans[g] * before[g]) / last_w
        for i, row in enumerate((first, last)):
            for j in range(per):
                spot = i * per + j
                back_ref[g, spot // 4, spot % 4 : spot % 4 + 1, :] = row[j : j + 1]


def final_kernel(
    got_ref, own_ref, thin_ref, x_ref, dual_ref, average_hbm, new_dual_hbm,
    first_ref, last_ref, average_ref, new_dual_ref, sems,
):
    owners = got_ref.shape[0]
    sections, nodes = first_ref.shape
    node_blocks = nodes // LANES
    per = sections * node_blocks // owners
    for owner in range(owners):
        block, col = owner // node_blocks, owner % node_blocks
        cols = slice(col * LANES, (col + 1) * LANES)
        for i, edge_ref in enumerate((first_ref, last_ref)):
            for j in range(per):
                spot, row = i * per + j, block * per + j
                edge_ref[row : row + 1, cols] = got_ref[owner, spot // 4, spot % 4 : spot % 4 + 1, :]
    leaves = x_ref.shape[0] // sections
    chunks = sems.shape[1]
    each = leaves // chunks
    copies = []
    for chunk in range(chunks):
        for i in range(chunk * each, (chunk + 1) * each):
            rows = slice(i * sections, (i + 1) * sections)
            offset = 2 * leaves * sections + i * sections
            pick = thin_ref[offset : offset + sections, :]
            for start in range(0, nodes, LANES):
                cols = slice(start, start + LANES)
                ends = jnp.where(pick > 1.5, last_ref[:, cols], first_ref[:, cols])
                average = jnp.where(pick > 0.5, ends, own_ref[rows, cols])
                average_ref[rows, cols] = average
                new_dual_ref[rows, cols] = dual_ref[rows, cols] + penalty * (
                    x_ref[rows, cols] - average
                )
        part = pl.ds(chunk * each * sections, each * sections)
        for n, (src, dst) in enumerate(((average_ref, average_hbm), (new_dual_ref, new_dual_hbm))):
            copy = pltpu.make_async_copy(src.at[part, :], dst.at[part, :], sems.at[n, chunk])
            copy.start()
            copies.append(copy)
    for copy in copies:
        copy.wait()


def call(kernel, inputs, outputs, in_specs=None, out_specs=None, scratch=(), name=None):
    return pl.pallas_call(
        kernel,
        out_shape=outputs,
        in_specs=in_specs or [VMEM] * len(inputs),
        out_specs=out_specs or jax.tree.map(lambda _: VMEM, outputs),
        scratch_shapes=scratch,
        compiler_params=PARAMS,
        name=name,
    )(*inputs)


def shaped(shape, dtype=jnp.float32):
    return jax.ShapeDtypeStruct(shape, dtype)


def gather_parts(part):
    spread = jnp.broadcast_to(part, (lax.axis_size("feeder"),) + part.shape)
    return lax.all_to_all(spread, "feeder", 0, 0)


def local(anchor, cost_lin, dual, target, leaf_weight, q_mat, diag_gain, block_mask, ancestor):
    leaves, sections, nodes = anchor.shape
    rows = leaves * sections
    groups = lax.axis_size("scen")
    total_nodes = lax.axis_size("feeder") * nodes
    flat = lambda a: a.reshape(rows, nodes)
    sums_shape = shaped((rows // LANES, LANES))
    full, small = shaped((rows, nodes)), shaped((3 * rows + sections + 8, LANES))
    buffer = pltpu.VMEM((rows, nodes), jnp.float32)
    edge = pltpu.VMEM((sections, nodes), jnp.float32)

    sums = call(
        sum_kernel,
        (flat(anchor),),
        sums_shape,
        in_specs=[HBM],
        scratch=(pltpu.VMEM((rows, nodes), jnp.bfloat16), pltpu.SemaphoreType.DMA((rows // LANES,))),
        name="start_sums",
    )
    got = gather_parts(sums)
    first_leaf = (lax.axis_index("scen") * leaves).astype(jnp.int32).reshape(1)
    q_eff, fixed, z, gain, dual_near, thin = call(
        prep_kernel,
        (first_leaf, leaf_weight, block_mask[0], target, ancestor.T, diag_gain.reshape(1, nodes),
         flat(anchor), flat(cost_lin), flat(dual), q_mat),
        (shaped((nodes, nodes), jnp.bfloat16), full, full, shaped((1, nodes)), full, small),
        in_specs=[SMEM] * 3 + [VMEM] * 3 + [HBM] * 4,
        scratch=(
            pltpu.VMEM((rows, nodes), jnp.bfloat16),
            pltpu.VMEM((rows, nodes), jnp.bfloat16),
            pltpu.VMEM((nodes, nodes), jnp.bfloat16),
            pltpu.SemaphoreType.DMA((4,)),
        ),
        name="prep",
    )
    for sweep in range(PROX_ITERS - 1):
        sums, z = call(
            lambda *refs: step_kernel(total_nodes, *refs),
            (got, z, q_eff, fixed, gain),
            (sums_shape, full),
            scratch=(buffer,),
            name="prox_step",
        )
        got = gather_parts(sums)
    x, own, sent = call(
        lambda *refs: last_kernel(total_nodes, *refs),
        (leaf_weight, got, z, thin),
        (full, full, shaped((groups, 16, LANES))),
        in_specs=[SMEM] + [VMEM] * 3,
        out_specs=(HBM, VMEM, VMEM),
        scratch=(buffer, edge, edge, pltpu.SemaphoreType.DMA),
        name="last_step",
    )
    per = sections * (nodes // LANES) // groups
    got = lax.all_to_all(sent, "scen", 0, 0)
    back = call(owner_kernel, (got,), shaped((groups, per // 2, 4, LANES)), name="owner_chain")
    got = lax.all_to_all(back, "scen", 0, 0)
    average, new_dual = call(
        final_kernel,
        (got, own, thin, x, dual_near),
        (full, full),
        out_specs=(HBM, HBM),
        scratch=(edge, edge, buffer, buffer, pltpu.SemaphoreType.DMA((2, 4))),
        name="finish",
    )
    whole = lambda a: a.reshape(leaves, sections, nodes)
    return (whole(x), whole(average), whole(new_dual))


def solution(mesh):
    return jax.shard_map(
        local,
        mesh=mesh,
        in_specs=(
            P("scen", None, "feeder"),
            P("scen", None, "feeder"),
            P("scen", None, "feeder"),
            P("scen", None),
            P("scen"),
            P("feeder", None),
            P("feeder"),
            P("feeder", None, None),
            P(None, "scen"),
        ),
        out_specs=(P("scen", None, "feeder"), P("scen", None, "feeder"), P("scen", None, "feeder")),
        check_vma=False,
    )
```

time: 156 us -> 153 us (0.981)
  blocking collectives: 131 us -> 126 us
  Pallas kernels: 7.61 us -> 9.22 us
    all_to_all x1, blocking collectives: 31.3 us -> 28.9 us  [local(): got = lax.all_to_all(sent, 'scen', 0, 0)]
    all_to_all x1, blocking collectives: 19.5 us -> 17.8 us  [local(): got = lax.all_to_all(back, 'scen', 0, 0)]
    pallas_call x12, Pallas kernels: 7.61 us -> 9.22 us  [call(): pl.pallas_call(kernel, out_shape=outputs, in_specs=in_specs or [VMEM] * l...]
  transfers between devices with their start and end apart: 1 -> 1, of which waited for: 0 -> 1; matrix products, arithmetic and copies ran while one was open for 1% -> 0% of each run, Pallas kernels for 1% -> 1%
where the time goes in v3:
time: 153 us; the launch traced here: 152 us
  blocking collectives  126 us (82%)
  Pallas kernels  9.22 us (6%)
  local copies, waits for them, and re-layouts  7.56 us (5%)
  starting transfers between devices  7.45 us (5%)
    all_to_all x7, blocking collectives, gather_parts(): return lax.all_to_all(spread, 'feeder', 0, 0)  79.2 us
    all_to_all x1, blocking collectives, local(): got = lax.all_to_all(sent, 'scen', 0, 0)  28.9 us
    all_to_all x1, blocking collectives, local(): got = lax.all_to_all(back, 'scen', 0, 0)  17.8 us
    pallas_call x12, Pallas kernels, call(): pl.pallas_call(kernel, out_shape=outputs, in_specs=in_specs or [VMEM] * l...  9.22 us
    all_to_all x1, starting transfers between devices, gather_parts(): return lax.all_to_all(spread, 'feeder', 0, 0)  7.45 us
    unnamed x26, local copies, waits for them, and re-layouts  6.84 us
  transfers between devices with their start and end apart: 1, of which 1 were waited for; matrix products, arithmetic and copies ran while one was open for 0% of the time, Pallas kernels for 1%

profile of v3, /device:TPU:32, one launch (start us, length us, event | category | flops | bytes accessed | tf_op | source)
XLA Modules:
  0.0 151.8 jit_solution(16380518806199017706)
XLA Ops:
  0.6 0.0 copy-start
  0.6 1.0 copy-done
  1.6 0.0 copy-start.1
  1.6 0.8 start_sums.1
  2.5 0.6 broadcast_in_dim.24
  3.1 0.0 copy-start.10
  3.1 0.0 copy-start.11
  3.1 7.5 %all-to-all-start = ((f32[32,3,128]{2,1,0:T(4,128)}), f32[32,3,128]{2,1,0:T(4,128)S(1)}, u32[]{:S(2)}, u32[]{:S(2)}) async-start(f32[32,3,128]{2,1,0:T(4,128)} %broadcast_in_dim.24), calls=%async_computation | async-start | bytes 131072 | tf_op jit(solution)/shard_map/all_to_all | solution.py:293
  10.6 0.0 copy-start.9
  10.6 0.0 copy-start.8
  10.6 0.0 copy-start.12
  10.6 0.0 copy-done.1
  10.6 0.0 copy-done.10
  10.6 0.0 copy-done.11
  10.7 0.6 copy-done.9
  11.3 0.0 copy-done.8
  11.3 0.0 copy-done.12
  11.3 0.0 copy-start.2
  11.3 1.1 copy-done.2
  12.4 0.0 copy-start.6
  12.4 1.0 copy-done.6
  13.5 0.0 copy-start.7
  13.5 1.0 copy-done.7
  14.5 2.0 %prep.1 = (bf16[512,512]{1,0:T(8,128)(2,1)S(1)}, f32[384,512]{1,0:T(8,128)S(1)}, f32[384,512]{1,0:T(8,128)S(1)}, f32[1,512]{1,0:T(1,128)S(1)}, f32[384,512]{1,0:T(8,128)S(1)}, /*index=5*/f32[1184,128]{1,0:T(8,128)S(1)}) custom-call(s32[1]{0:T(128)} %bitcast.1.first_ref, f32[16]{0:T(128)S(1)} %copy-done.12, s32[4,4]{1,0:T(4,128)S(1)} %bitcast.16, ...), custom_call_target="tpu_custom_call" | custom-call | tf_op jit(solution)/shard_map/prep/pallas_call | solution.py:276
  16.5 0.0 copy-start.3
  16.5 0.9 copy-done.3
  17.4 0.7 all-to-all-done.refs_0_
  18.1 0.5 prox_step.7
  18.6 14.0 %all_to_all.50.refs_0_ = f32[32,3,128]{2,1,0:T(4,128)S(1)} all-to-all(f32[32,3,128]{2,1,0:T(4,128)S(1)} %broadcast_in_dim.25), channel_id=1, replica_groups=mesh['feeder'=32,'scen'=16] {'feeder'}, dimensions={0} | all-to-all | bytes 98304 | tf_op jit(solution)/shard_map/all_to_all | solution.py:293
  32.6 0.5 prox_step.8
  33.1 10.9 %all_to_all.51.refs_0_ = f32[32,3,128]{2,1,0:T(4,128)S(1)} all-to-all(f32[32,3,128]{2,1,0:T(4,128)S(1)} %broadcast_in_dim.26), channel_id=1, replica_groups=mesh['feeder'=32,'scen'=16] {'feeder'}, dimensions={0} | all-to-all | bytes 98304 | tf_op jit(solution)/shard_map/all_to_all | solution.py:293
  43.9 0.5 prox_step.9
  44.4 10.9 %all_to_all.52.refs_0_ = f32[32,3,128]{2,1,0:T(4,128)S(1)} all-to-all(f32[32,3,128]{2,1,0:T(4,128)S(1)} %broadcast_in_dim.27), channel_id=1, replica_groups=mesh['feeder'=32,'scen'=16] {'feeder'}, dimensions={0} | all-to-all | bytes 98304 | tf_op jit(solution)/shard_map/all_to_all | solution.py:293
  55.3 0.5 prox_step.10
  55.8 10.9 %all_to_all.53.refs_0_ = f32[32,3,128]{2,1,0:T(4,128)S(1)} all-to-all(f32[32,3,128]{2,1,0:T(4,128)S(1)} %broadcast_in_dim.28), channel_id=1, replica_groups=mesh['feeder'=32,'scen'=16] {'feeder'}, dimensions={0} | all-to-all | bytes 98304 | tf_op jit(solution)/shard_map/all_to_all | solution.py:293
  66.7 0.5 prox_step.11
  67.1 10.9 %all_to_all.54.refs_0_ = f32[32,3,128]{2,1,0:T(4,128)S(1)} all-to-all(f32[32,3,128]{2,1,0:T(4,128)S(1)} %broadcast_in_dim.29), channel_id=1, replica_groups=mesh['feeder'=32,'scen'=16] {'feeder'}, dimensions={0} | all-to-all | bytes 98304 | tf_op jit(solution)/shard_map/all_to_all | solution.py:293
  78.0 0.5 prox_step.12
  78.5 10.9 %all_to_all.55.refs_0_ = f32[32,3,128]{2,1,0:T(4,128)S(1)} all-to-all(f32[32,3,128]{2,1,0:T(4,128)S(1)} %broadcast_in_dim.30), channel_id=1, replica_groups=mesh['feeder'=32,'scen'=16] {'feeder'}, dimensions={0} | all-to-all | bytes 98304 | tf_op jit(solution)/shard_map/all_to_all | solution.py:293
  89.4 0.5 prox_step.13
  89.8 10.9 %all_to_all.56.refs_1_ = f32[32,3,128]{2,1,0:T(4,128)S(1)} all-to-all(f32[32,3,128]{2,1,0:T(4,128)S(1)} %broadcast_in_dim.31), channel_id=1, replica_groups=mesh['feeder'=32,'scen'=16] {'feeder'}, dimensions={0} | all-to-all | bytes 98304 | tf_op jit(solution)/shard_map/all_to_all | solution.py:293
  100.7 0.0 copy-start.4
  100.7 1.7 %last_step.1 = (f32[384,512]{1,0:T(8,128)}, f32[384,512]{1,0:T(8,128)S(1)}, f32[16,16,128]{2,1,0:T(8,128)S(1)}) custom-call(f32[16]{0:T(128)S(1)} %copy-done.12, f32[32,3,128]{2,1,0:T(4,128)S(1)} %all_to_all.56.refs_1_, f32[384,512]{1,0:T(8,128)S(1)} %get-tuple-element.45.refs_2_, f32[1184,128]{1,0:T(8,128)S(1)} %get-tuple-element.46.refs_3_.thin_ref), custom_call_target="tpu_custom_call" | custom-call | tf_op jit(solution)/shard_map/last_step/pallas_call | solution.py:276
  102.5 28.9 %all_to_all.57.got_ref = f32[16,16,128]{2,1,0:T(8,128)S(1)} all-to-all(f32[16,16,128]{2,1,0:T(8,128)S(1)} %get-tuple-element.48), channel_id=1, replica_groups=mesh['feeder'=32,'scen'=16] {'scen'}, dimensions={0} | all-to-all | bytes 262144 | tf_op jit(solution)/shard_map/all_to_all | solution.py:350
  131.4 0.2 owner_chain.1
  131.6 17.8 %all_to_all.58.got_ref = f32[16,3,4,128]{3,2,1,0:T(4,128)S(1)} all-to-all(f32[16,3,4,128]{3,2,1,0:T(4,128)S(1)} %owner_chain.1), channel_id=1, replica_groups=mesh['feeder'=32,'scen'=16] {'scen'}, dimensions={0} | all-to-all | bytes 196608 | tf_op jit(solution)/shard_map/all_to_all | solution.py:352
  149.4 0.0 copy-done.4
  149.4 0.0 copy-start.5
  149.4 1.1 copy-done.5
  150.5 1.3 finish.1
  (7 shorter events, 0.1 us)
Async XLA Ops:
  0.6 1.0 copy-start
  1.6 9.0 %copy-start.1 = (bf16[16,24,512]{2,1,0:T(8,128)(2,1)S(1)}, bf16[16,24,512]{2,1,0:T(8,128)(2,1)}, u32[]{:S(2)}) copy-start(bf16[16,24,512]{2,1,0:T(8,128)(2,1)} %param.9) | copy-start | bytes 1179652
  3.1 7.5 %copy-start.10 = (s32[1,4,4]{2,1,0:T(4,128)S(1)}, s32[1,4,4]{2,1,0:T(4,128)}, u32[]{:S(2)}) copy-start(s32[1,4,4]{2,1,0:T(4,128)} %param.16) | copy-start | bytes 196
  3.1 7.5 %copy-start.11 = (f32[512]{0:T(512)S(1)}, f32[512]{0:T(512)}, u32[]{:S(2)}) copy-start(f32[512]{0:T(512)} %param.15) | copy-start | bytes 6148
  3.1 15.0 %all-to-all-start = ((f32[32,3,128]{2,1,0:T(4,128)}), f32[32,3,128]{2,1,0:T(4,128)S(1)}, u32[]{:S(2)}, u32[]{:S(2)}) async-start(f32[32,3,128]{2,1,0:T(4,128)} %broadcast_in_dim.24), calls=%async_computation | async-start | bytes 131072 | tf_op jit(solution)/shard_map/all_to_all | solution.py:293
  10.6 0.7 copy-start.9
  10.6 0.7 copy-start.8
  10.6 0.7 copy-start.12
  11.3 1.1 copy-start.2
  12.4 1.0 copy-start.6
  13.5 1.0 copy-start.7
  16.5 0.9 copy-start.3
  100.7 48.6 %copy-start.4 = (f32[384,512]{1,0:T(8,128)S(1)}, f32[384,512]{1,0:T(8,128)}, u32[]{:S(2)}) copy-start(f32[384,512]{1,0:T(8,128)} %copy-done.3) | copy-start | bytes 2359300
  149.4 1.1 copy-start.5

commit v4 on v3

--- a/solution.py
+++ b/solution.py
@@ -18,6 +18,7 @@
 SMEM = pl.BlockSpec(memory_space=pltpu.SMEM)
 HBM = pl.BlockSpec(memory_space=pltpu.HBM)
 PARAMS = pltpu.CompilerParams(vmem_limit_bytes=12 * 1024 * 1024)
+PREP_PARAMS = pltpu.CompilerParams()
 
 
 def row_sums(block):
@@ -25,20 +26,6 @@
     for start in range(LANES, block.shape[1], LANES):
         total = total + block[:, start : start + LANES]
     return jnp.sum(total.T, axis=0, keepdims=True)
-
-
-def sum_kernel(anchor_hbm, sums_ref, anchor_ref, sems):
-    copies = []
-    for i in range(anchor_ref.shape[0] // LANES):
-        part = pl.ds(i * LANES, LANES)
-        copies.append(
-            pltpu.make_async_copy(anchor_hbm.at[part, :], anchor_ref.at[part, :], sems.at[i])
-        )
-        copies[i].start()
-    for i in range(anchor_ref.shape[0] // LANES):
-        copies[i].wait()
-        block = anchor_ref[i * LANES : (i + 1) * LANES, :].astype(jnp.float32)
-        sums_ref[i : i + 1, :] = row_sums(block)
 
 
 def affine(x, image, gain, fixed):
@@ -56,10 +43,10 @@
 def prep_kernel(
     first_ref, weight_ref, mask_ref, target_ref, anc_ref, diag_ref,
     anchor_hbm, cost_hbm, dual_hbm, q_hbm,
-    q_out, fixed_out, z_out, gain_out, dual_out, thin_out,
-    anchor_ref, cost_ref, q_ref, sems,
+    sums_ref, q_out, fixed_out, z_out, gain_out, thin_out,
+    anchor_ref, cost_ref, dual_ref, q_ref, sems,
 ):
-    moves = ((q_hbm, q_ref), (anchor_hbm, anchor_ref), (cost_hbm, cost_ref), (dual_hbm, dual_out))
+    moves = ((anchor_hbm, anchor_ref), (q_hbm, q_ref), (cost_hbm, cost_ref), (dual_hbm, dual_ref))
     copies = [pltpu.make_async_copy(src, dst, sems.at[i]) for i, (src, dst) in enumerate(moves)]
     for copy in copies:
         copy.start()
@@ -107,12 +94,15 @@
     count = mask_ref.shape[0]
     width = q_ref.shape[0] // count
     copies[0].wait()
+    for i in range(rows_all // LANES):
+        block = anchor_ref[i * LANES : (i + 1) * LANES, :].astype(jnp.float32)
+        sums_ref[i : i + 1, :] = row_sums(block)
+    copies[1].wait()
     for i in range(count):
         for j in range(count):
             rows, cols = slice(i * width, (i + 1) * width), slice(j * width, (j + 1) * width)
             keep = mask_ref[i, j].astype(jnp.float32).astype(jnp.bfloat16)
             q_out[rows, cols] = q_ref[rows, cols] * keep
-    copies[1].wait()
     image = jnp.dot(anchor_ref[...], q_out[...], preferred_element_type=jnp.float32)
     z_out[...] = image
     copies[2].wait()
@@ -121,7 +111,7 @@
         rows = slice(i * sections, (i + 1) * sections)
         pull = (step_size * coupling) * column(target_ref[i : i + 1, :])
         start_pt = anchor_ref[rows, :].astype(jnp.float32)
-        linear = cost_ref[rows, :].astype(jnp.float32) + dual_out[rows, :] - penalty * start_pt
+        linear = cost_ref[rows, :].astype(jnp.float32) + dual_ref[rows, :] - penalty * start_pt
         fixed = step_size * linear - pull
         fixed_out[rows, :] = fixed
         z_out[rows, :] = affine(start_pt, z_out[rows, :], gain, fixed)
@@ -150,12 +140,9 @@
 
 def last_kernel(
     total_nodes, weight_ref, got_ref, z_ref, thin_ref,
-    x_hbm, own_ref, sent_ref,
-    x_ref, tail_ref, head_ref, sem,
+    x_ref, own_ref, sent_ref, tail_ref, head_ref,
 ):
     clipped(total_nodes, got_ref, z_ref, x_ref)
-    copy = pltpu.make_async_copy(x_ref, x_hbm, sem)
-    copy.start()
     leaves = weight_ref.shape[0]
     rows_all, nodes = x_ref.shape
     sections = rows_all // leaves
@@ -190,7 +177,6 @@
         sent_ref[owner, per : per + 1, :] = thin_ref[spot : spot + 1, :]
         sent_ref[owner, 8 : 8 + per, :] = head_ref[rows, cols]
         sent_ref[owner, 8 + per : 16, :] = zeros
-    copy.wait()
 
 
 def owner_kernel(got_ref, back_ref):
@@ -232,9 +218,11 @@
 
 
 def final_kernel(
-    got_ref, own_ref, thin_ref, x_ref, dual_ref, average_hbm, new_dual_hbm,
-    first_ref, last_ref, average_ref, new_dual_ref, sems,
+    got_ref, own_ref, thin_ref, x_ref, dual_ref, x_hbm, average_hbm, new_dual_hbm,
+    first_ref, last_ref, average_ref, new_dual_ref, sems, x_sem,
 ):
+    copies = [pltpu.make_async_copy(x_ref, x_hbm, x_sem)]
+    copies[0].start()
     owners = got_ref.shape[0]
     sections, nodes = first_ref.shape
     node_blocks = nodes // LANES
@@ -249,7 +237,6 @@
     leaves = x_ref.shape[0] // sections
     chunks = sems.shape[1]
     each = leaves // chunks
-    copies = []
     for chunk in range(chunks):
         for i in range(chunk * each, (chunk + 1) * each):
             rows = slice(i * sections, (i + 1) * sections)
@@ -272,14 +259,14 @@
         copy.wait()
 
 
-def call(kernel, inputs, outputs, in_specs=None, out_specs=None, scratch=(), name=None):
+def call(kernel, inputs, outputs, in_specs=None, out_specs=None, scratch=(), params=PARAMS, name=None):
     return pl.pallas_call(
         kernel,
         out_shape=outputs,
         in_specs=in_specs or [VMEM] * len(inputs),
         out_specs=out_specs or jax.tree.map(lambda _: VMEM, outputs),
         scratch_shapes=scratch,
-        compiler_params=PARAMS,
+        compiler_params=params,
         name=name,
     )(*inputs)
 
@@ -304,30 +291,22 @@
     buffer = pltpu.VMEM((rows, nodes), jnp.float32)
     edge = pltpu.VMEM((sections, nodes), jnp.float32)
 
-    sums = call(
-        sum_kernel,
-        (flat(anchor),),
-        sums_shape,
-        in_specs=[HBM],
-        scratch=(pltpu.VMEM((rows, nodes), jnp.bfloat16), pltpu.SemaphoreType.DMA((rows // LANES,))),
-        name="start_sums",
-    )
-    got = gather_parts(sums)
     first_leaf = (lax.axis_index("scen") * leaves).astype(jnp.int32).reshape(1)
-    q_eff, fixed, z, gain, dual_near, thin = call(
+    narrow = pltpu.VMEM((rows, nodes), jnp.bfloat16)
+    sums, q_eff, fixed, z, gain, thin = call(
         prep_kernel,
         (first_leaf, leaf_weight, block_mask[0], target, ancestor.T, diag_gain.reshape(1, nodes),
          flat(anchor), flat(cost_lin), flat(dual), q_mat),
-        (shaped((nodes, nodes), jnp.bfloat16), full, full, shaped((1, nodes)), full, small),
+        (sums_shape, shaped((nodes, nodes), jnp.bfloat16), full, full, shaped((1, nodes)), small),
         in_specs=[SMEM] * 3 + [VMEM] * 3 + [HBM] * 4,
         scratch=(
-            pltpu.VMEM((rows, nodes), jnp.bfloat16),
-            pltpu.VMEM((rows, nodes), jnp.bfloat16),
-            pltpu.VMEM((nodes, nodes), jnp.bfloat16),
+            narrow, narrow, buffer, pltpu.VMEM((nodes, nodes), jnp.bfloat16),
             pltpu.SemaphoreType.DMA((4,)),
         ),
+        params=PREP_PARAMS,
         name="prep",
     )
+    got = gather_parts(sums)
     for sweep in range(PROX_ITERS - 1):
         sums, z = call(
             lambda *refs: step_kernel(total_nodes, *refs),
@@ -342,20 +321,21 @@
         (leaf_weight, got, z, thin),
         (full, full, shaped((groups, 16, LANES))),
         in_specs=[SMEM] + [VMEM] * 3,
-        out_specs=(HBM, VMEM, VMEM),
-        scratch=(buffer, edge, edge, pltpu.SemaphoreType.DMA),
+        scratch=(edge, edge),
         name="last_step",
     )
     per = sections * (nodes // LANES) // groups
     got = lax.all_to_all(sent, "scen", 0, 0)
     back = call(owner_kernel, (got,), shaped((groups, per // 2, 4, LANES)), name="owner_chain")
     got = lax.all_to_all(back, "scen", 0, 0)
-    average, new_dual = call(
+    x, average, new_dual = call(
         final_kernel,
-        (got, own, thin, x, dual_near),
-        (full, full),
-        out_specs=(HBM, HBM),
-        scratch=(edge, edge, buffer, buffer, pltpu.SemaphoreType.DMA((2, 4))),
+        (got, own, thin, x, flat(dual)),
+        (full, full, full),
+        out_specs=(HBM, HBM, HBM),
+        scratch=(
+            edge, edge, buffer, buffer, pltpu.SemaphoreType.DMA((2, 4)), pltpu.SemaphoreType.DMA
+        ),
         name="finish",
     )
     whole = lambda a: a.reshape(leaves, sections, nodes)

time: 153 us -> 154 us (level)
  blocking collectives: 126 us -> 137 us
  starting transfers between devices: 7.45 us -> 0 us
  local copies, waits for them, and re-layouts: 7.56 us -> 5.38 us
    all_to_all x7 -> x8, blocking collectives: 79.2 us -> 90.7 us  [gather_parts(): return lax.all_to_all(spread, 'feeder', 0, 0)]
    all_to_all x1 -> x0, starting transfers between devices: 7.45 us -> none  [gather_parts(): return lax.all_to_all(spread, 'feeder', 0, 0)]
    unnamed x26 -> x14, local copies, waits for them, and re-layouts: 6.84 us -> 4.62 us
    pallas_call x12 -> x11, Pallas kernels: 9.22 us -> 9.77 us  [call(): pl.pallas_call(kernel, out_shape=outputs, in_specs=in_specs or [VMEM] * l...]
  transfers between devices with their start and end apart: 1 -> 0, of which waited for: 1 -> 0; matrix products, arithmetic and copies ran while one was open for 0% -> 0% of each run, Pallas kernels for 1% -> 0%
where the time goes in v4:
time: 154 us; the launch traced here: 153 us
  blocking collectives  137 us (89%)
  Pallas kernels  9.77 us (6%)
  local copies, waits for them, and re-layouts  5.38 us (3%)
    all_to_all x8, blocking collectives, gather_parts(): return lax.all_to_all(spread, 'feeder', 0, 0)  90.7 us
    all_to_all x1, blocking collectives, local(): got = lax.all_to_all(sent, 'scen', 0, 0)  28.9 us
    all_to_all x1, blocking collectives, local(): got = lax.all_to_all(back, 'scen', 0, 0)  17.8 us
    pallas_call x11, Pallas kernels, call(): pl.pallas_call(kernel, out_shape=outputs, in_specs=in_specs or [VMEM] * l...  9.77 us
    unnamed x14, local copies, waits for them, and re-layouts  4.62 us

profile of v4, /device:TPU:32, one launch (start us, length us, event | category | flops | bytes accessed | tf_op | source)
XLA Modules:
  0.0 153.4 jit_solution(12799557444077455782)
XLA Ops:
  0.6 4.0 %prep.1 = (f32[3,128]{1,0:T(4,128)}, bf16[512,512]{1,0:T(8,128)(2,1)}, f32[384,512]{1,0:T(8,128)}, f32[384,512]{1,0:T(8,128)}, f32[1,512]{1,0:T(1,128)}, /*index=5*/f32[1184,128]{1,0:T(8,128)}) custom-call(s32[1]{0:T(128)} %bitcast.first_ref, f32[16]{0:T(128)} %refs_0_.1, s32[4,4]{1,0:T(4,128)} %bitcast.15, f32[16,24]{1,0:T(8,128)} %target_ref.1, ...), custom_call_target="tpu_custom_call" | custom-call | tf_op jit(solution)/shard_map/prep/pallas_call | solution.py:263
  4.7 0.7 broadcast_in_dim.24
  5.3 14.6 %all_to_all.50.refs_0_ = f32[32,3,128]{2,1,0:T(4,128)S(1)} all-to-all(f32[32,3,128]{2,1,0:T(4,128)S(1)} %broadcast_in_dim.24), channel_id=1, replica_groups=mesh['feeder'=32,'scen'=16] {'feeder'}, dimensions={0} | all-to-all | bytes 98304 | tf_op jit(solution)/shard_map/all_to_all | solution.py:280
  20.0 0.0 copy-start.5
  20.0 0.7 copy-done.5
  20.6 0.0 copy-start
  20.6 1.1 copy-done
  21.8 0.0 copy-start.1
  21.8 1.0 copy-done.1
  22.8 0.0 copy-start.4
  22.8 1.1 copy-done.4
  24.0 0.5 prox_step.7
  24.4 10.9 %all_to_all.51.refs_0_ = f32[32,3,128]{2,1,0:T(4,128)S(1)} all-to-all(f32[32,3,128]{2,1,0:T(4,128)S(1)} %broadcast_in_dim.25), channel_id=1, replica_groups=mesh['feeder'=32,'scen'=16] {'feeder'}, dimensions={0} | all-to-all | bytes 98304 | tf_op jit(solution)/shard_map/all_to_all | solution.py:280
  35.3 0.5 prox_step.8
  35.8 10.9 %all_to_all.52.refs_0_ = f32[32,3,128]{2,1,0:T(4,128)S(1)} all-to-all(f32[32,3,128]{2,1,0:T(4,128)S(1)} %broadcast_in_dim.26), channel_id=1, replica_groups=mesh['feeder'=32,'scen'=16] {'feeder'}, dimensions={0} | all-to-all | bytes 98304 | tf_op jit(solution)/shard_map/all_to_all | solution.py:280
  46.7 0.5 prox_step.9
  47.2 10.9 %all_to_all.53.refs_0_ = f32[32,3,128]{2,1,0:T(4,128)S(1)} all-to-all(f32[32,3,128]{2,1,0:T(4,128)S(1)} %broadcast_in_dim.27), channel_id=1, replica_groups=mesh['feeder'=32,'scen'=16] {'feeder'}, dimensions={0} | all-to-all | bytes 98304 | tf_op jit(solution)/shard_map/all_to_all | solution.py:280
  58.0 0.5 prox_step.10
  58.5 10.9 %all_to_all.54.refs_0_ = f32[32,3,128]{2,1,0:T(4,128)S(1)} all-to-all(f32[32,3,128]{2,1,0:T(4,128)S(1)} %broadcast_in_dim.28), channel_id=1, replica_groups=mesh['feeder'=32,'scen'=16] {'feeder'}, dimensions={0} | all-to-all | bytes 98304 | tf_op jit(solution)/shard_map/all_to_all | solution.py:280
  69.4 0.5 prox_step.11
  69.9 10.9 %all_to_all.55.refs_0_ = f32[32,3,128]{2,1,0:T(4,128)S(1)} all-to-all(f32[32,3,128]{2,1,0:T(4,128)S(1)} %broadcast_in_dim.29), channel_id=1, replica_groups=mesh['feeder'=32,'scen'=16] {'feeder'}, dimensions={0} | all-to-all | bytes 98304 | tf_op jit(solution)/shard_map/all_to_all | solution.py:280
  80.8 0.5 prox_step.12
  81.2 10.9 %all_to_all.56.refs_0_ = f32[32,3,128]{2,1,0:T(4,128)S(1)} all-to-all(f32[32,3,128]{2,1,0:T(4,128)S(1)} %broadcast_in_dim.30), channel_id=1, replica_groups=mesh['feeder'=32,'scen'=16] {'feeder'}, dimensions={0} | all-to-all | bytes 98304 | tf_op jit(solution)/shard_map/all_to_all | solution.py:280
  92.1 0.0 copy-start.3
  92.1 0.5 prox_step.13
  92.6 10.9 %all_to_all.57.refs_1_ = f32[32,3,128]{2,1,0:T(4,128)S(1)} all-to-all(f32[32,3,128]{2,1,0:T(4,128)S(1)} %broadcast_in_dim.31), channel_id=1, replica_groups=mesh['feeder'=32,'scen'=16] {'feeder'}, dimensions={0} | all-to-all | bytes 98304 | tf_op jit(solution)/shard_map/all_to_all | solution.py:280
  103.5 0.0 copy-start.6
  103.5 0.0 copy-done.3
  103.5 0.7 copy-done.6
  104.1 0.0 copy-start.2
  104.1 0.9 last_step.1
  105.0 28.9 %all_to_all.58.got_ref = f32[16,16,128]{2,1,0:T(8,128)S(1)} all-to-all(f32[16,16,128]{2,1,0:T(8,128)S(1)} %get-tuple-element.49), channel_id=1, replica_groups=mesh['feeder'=32,'scen'=16] {'scen'}, dimensions={0} | all-to-all | bytes 262144 | tf_op jit(solution)/shard_map/all_to_all | solution.py:328
  133.9 0.2 owner_chain.1
  134.1 17.8 %all_to_all.59.got_ref = f32[16,3,4,128]{3,2,1,0:T(4,128)S(1)} all-to-all(f32[16,3,4,128]{3,2,1,0:T(4,128)S(1)} %owner_chain.1), channel_id=1, replica_groups=mesh['feeder'=32,'scen'=16] {'scen'}, dimensions={0} | all-to-all | bytes 196608 | tf_op jit(solution)/shard_map/all_to_all | solution.py:330
  151.9 0.0 copy-done.2
  151.9 1.5 finish.1
  (7 shorter events, 0.1 us)
Async XLA Ops:
  20.0 0.7 copy-start.5
  20.6 1.1 copy-start
  21.8 1.0 copy-start.1
  22.8 1.1 copy-start.4
  92.1 11.4 %copy-start.3 = (f32[1184,128]{1,0:T(8,128)S(1)}, f32[1184,128]{1,0:T(8,128)}, u32[]{:S(2)}) copy-start(f32[1184,128]{1,0:T(8,128)} %get-tuple-element.48.refs_3_.thin_ref) | copy-start | bytes 1818628
  103.5 0.7 copy-start.6
  104.1 47.8 %copy-start.2 = (f32[16,24,512]{2,1,0:T(8,128)S(1)}, f32[16,24,512]{2,1,0:T(8,128)}, u32[]{:S(2)}) copy-start(f32[16,24,512]{2,1,0:T(8,128)} %param.11) | copy-start | bytes 2359300

commit v5 on v4

--- a/solution.py
+++ b/solution.py
@@ -18,7 +18,6 @@
 SMEM = pl.BlockSpec(memory_space=pltpu.SMEM)
 HBM = pl.BlockSpec(memory_space=pltpu.HBM)
 PARAMS = pltpu.CompilerParams(vmem_limit_bytes=12 * 1024 * 1024)
-PREP_PARAMS = pltpu.CompilerParams()
 
 
 def row_sums(block):
@@ -26,6 +25,23 @@
     for start in range(LANES, block.shape[1], LANES):
         total = total + block[:, start : start + LANES]
     return jnp.sum(total.T, axis=0, keepdims=True)
+
+
+def fetch(pairs, sems):
+    copies = [pltpu.make_async_copy(src, dst, sems.at[i]) for i, (src, dst) in enumerate(pairs)]
+    for copy in copies:
+        copy.start()
+    return copies
+
+
+def sum_kernel(anchor_hbm, spread_ref, anchor_ref, sems):
+    parts = [pl.ds(i * LANES, LANES) for i in range(anchor_ref.shape[0] // LANES)]
+    copies = fetch([(anchor_hbm.at[part, :], anchor_ref.at[part, :]) for part in parts], sems)
+    for i, part in enumerate(parts):
+        copies[i].wait()
+        total = row_sums(anchor_ref[part, :].astype(jnp.float32))
+        for feeder in range(spread_ref.shape[0]):
+            spread_ref[feeder, i : i + 1, :] = total
 
 
 def affine(x, image, gain, fixed):
@@ -41,15 +57,21 @@
 
 
 def prep_kernel(
-    first_ref, weight_ref, mask_ref, target_ref, anc_ref, diag_ref,
-    anchor_hbm, cost_hbm, dual_hbm, q_hbm,
-    sums_ref, q_out, fixed_out, z_out, gain_out, thin_out,
-    anchor_ref, cost_ref, dual_ref, q_ref, sems,
+    first_ref, target_hbm, anc_hbm, weight_hbm, mask_hbm, diag_hbm,
+    q_hbm, anchor_hbm, cost_hbm, dual_hbm,
+    q_out, fixed_out, z_out, gain_out, thin_out,
+    target_ref, anc_ref, weight_ref, mask_ref, diag_ref,
+    q_ref, anchor_ref, cost_ref, dual_ref, sems,
 ):
-    moves = ((anchor_hbm, anchor_ref), (q_hbm, q_ref), (cost_hbm, cost_ref), (dual_hbm, dual_ref))
-    copies = [pltpu.make_async_copy(src, dst, sems.at[i]) for i, (src, dst) in enumerate(moves)]
-    for copy in copies:
-        copy.start()
+    sources = (
+        anc_hbm, weight_hbm, mask_hbm, diag_hbm, target_hbm, q_hbm, anchor_hbm, cost_hbm, dual_hbm
+    )
+    places = (
+        anc_ref, weight_ref, mask_ref, diag_ref, target_ref, q_ref, anchor_ref, cost_ref, dual_ref
+    )
+    copies = fetch(list(zip(sources, places)), sems)
+    copies[0].wait()
+    copies[1].wait()
     leaves, sections = anc_ref.shape
     rows_all = leaves * sections
     thin = (sections, LANES)
@@ -58,7 +80,8 @@
     anc = [jnp.broadcast_to(column(owner_of[i : i + 1, :]), thin) for i in range(leaves)]
     run, same = [], []
     for i in range(leaves):
-        weight = jnp.full(thin, weight_ref[i], jnp.float32)
+        weight = jnp.broadcast_to(weight_ref[:, i : i + 1], thin)
+        thin_out[3 * rows_all + i * sections : 3 * rows_all + (i + 1) * sections, :] = weight
         same.append(jnp.where(anc[i] == anc[i - 1], 1.0, 0.0) if i else jnp.zeros(thin, jnp.float32))
         run.append(weight + same[i] * run[-1] if i else weight)
     for i in reversed(range(leaves - 1)):
@@ -73,7 +96,7 @@
         )
     cont = jnp.where(anc[0] < first_leaf, 1.0, 0.0)
     span = jnp.where(anc[-1] < first_leaf, 1.0, 0.0)
-    end = 3 * rows_all
+    end = 4 * rows_all
     thin_out[end : end + sections, :] = cont
     blocks = 8
     per = sections // 4
@@ -88,25 +111,26 @@
         spot = end + sections + block
         thin_out[spot : spot + 1, :] = jnp.sum(line, axis=0, keepdims=True)
     thin_out[end + sections + 4 : end + sections + blocks, :] = jnp.zeros((4, LANES), jnp.float32)
+    copies[2].wait()
+    copies[3].wait()
+    copies[4].wait()
     gain = 1.0 - step_size * (2.0 * diag_ref[...] + penalty)
     gain_out[...] = gain
 
     count = mask_ref.shape[0]
     width = q_ref.shape[0] // count
-    copies[0].wait()
-    for i in range(rows_all // LANES):
-        block = anchor_ref[i * LANES : (i + 1) * LANES, :].astype(jnp.float32)
-        sums_ref[i : i + 1, :] = row_sums(block)
-    copies[1].wait()
+    keep = mask_ref[...].astype(jnp.float32)
+    copies[5].wait()
     for i in range(count):
         for j in range(count):
             rows, cols = slice(i * width, (i + 1) * width), slice(j * width, (j + 1) * width)
-            keep = mask_ref[i, j].astype(jnp.float32).astype(jnp.bfloat16)
-            q_out[rows, cols] = q_ref[rows, cols] * keep
+            block = jnp.broadcast_to(keep[i : i + 1, j : j + 1], (width, width))
+            q_out[rows, cols] = q_ref[rows, cols] * block.astype(jnp.bfloat16)
+    copies[6].wait()
     image = jnp.dot(anchor_ref[...], q_out[...], preferred_element_type=jnp.float32)
     z_out[...] = image
-    copies[2].wait()
-    copies[3].wait()
+    copies[7].wait()
+    copies[8].wait()
     for i in range(leaves):
         rows = slice(i * sections, (i + 1) * sections)
         pull = (step_size * coupling) * column(target_ref[i : i + 1, :])
@@ -139,23 +163,23 @@
 
 
 def last_kernel(
-    total_nodes, weight_ref, got_ref, z_ref, thin_ref,
+    total_nodes, leaves, got_ref, z_ref, thin_ref,
     x_ref, own_ref, sent_ref, tail_ref, head_ref,
 ):
     clipped(total_nodes, got_ref, z_ref, x_ref)
-    leaves = weight_ref.shape[0]
     rows_all, nodes = x_ref.shape
     sections = rows_all // leaves
     owners = sent_ref.shape[0]
     node_blocks = nodes // LANES
     per = sections * node_blocks // owners
-    end = 3 * rows_all
+    end = 4 * rows_all
     for start in range(0, nodes, LANES):
         cols = slice(start, start + LANES)
         run = []
         for i in range(leaves):
             rows = slice(i * sections, (i + 1) * sections)
-            term = weight_ref[i] * x_ref[rows, cols]
+            mine = slice(3 * rows_all + i * sections, 3 * rows_all + (i + 1) * sections)
+            term = thin_ref[mine, :] * x_ref[rows, cols]
             run.append(term if i == 0 else term + thin_ref[rows, :] * run[-1])
         total = run[-1]
         tail_ref[:, cols] = total
@@ -259,20 +283,24 @@
         copy.wait()
 
 
-def call(kernel, inputs, outputs, in_specs=None, out_specs=None, scratch=(), params=PARAMS, name=None):
+def call(kernel, inputs, outputs, in_specs=None, out_specs=None, scratch=(), name=None):
     return pl.pallas_call(
         kernel,
         out_shape=outputs,
         in_specs=in_specs or [VMEM] * len(inputs),
         out_specs=out_specs or jax.tree.map(lambda _: VMEM, outputs),
         scratch_shapes=scratch,
-        compiler_params=params,
+        compiler_params=PARAMS,
         name=name,
     )(*inputs)
 
 
 def shaped(shape, dtype=jnp.float32):
     return jax.ShapeDtypeStruct(shape, dtype)
+
+
+def far(array):
+    return pltpu.with_memory_space_constraint(array, pltpu.HBM)
 
 
 def gather_parts(part):
@@ -287,26 +315,35 @@
     total_nodes = lax.axis_size("feeder") * nodes
     flat = lambda a: a.reshape(rows, nodes)
     sums_shape = shaped((rows // LANES, LANES))
-    full, small = shaped((rows, nodes)), shaped((3 * rows + sections + 8, LANES))
+    full, small = shaped((rows, nodes)), shaped((4 * rows + sections + 8, LANES))
     buffer = pltpu.VMEM((rows, nodes), jnp.float32)
     edge = pltpu.VMEM((sections, nodes), jnp.float32)
 
+    narrow = pltpu.VMEM((rows, nodes), jnp.bfloat16)
+    spread = call(
+        sum_kernel,
+        (far(flat(anchor)),),
+        shaped((lax.axis_size("feeder"),) + sums_shape.shape),
+        in_specs=[HBM],
+        scratch=(narrow, pltpu.SemaphoreType.DMA((rows // LANES,))),
+        name="start_sums",
+    )
+    got = lax.all_to_all(spread, "feeder", 0, 0)
     first_leaf = (lax.axis_index("scen") * leaves).astype(jnp.int32).reshape(1)
-    narrow = pltpu.VMEM((rows, nodes), jnp.bfloat16)
-    sums, q_eff, fixed, z, gain, thin = call(
+    small_args = (
+        target, ancestor.T, leaf_weight.reshape(1, leaves), block_mask[0],
+        diag_gain.reshape(1, nodes),
+    )
+    large_args = (q_mat, flat(anchor), flat(cost_lin), flat(dual))
+    q_eff, fixed, z, gain, thin = call(
         prep_kernel,
-        (first_leaf, leaf_weight, block_mask[0], target, ancestor.T, diag_gain.reshape(1, nodes),
-         flat(anchor), flat(cost_lin), flat(dual), q_mat),
-        (sums_shape, shaped((nodes, nodes), jnp.bfloat16), full, full, shaped((1, nodes)), small),
-        in_specs=[SMEM] * 3 + [VMEM] * 3 + [HBM] * 4,
-        scratch=(
-            narrow, narrow, buffer, pltpu.VMEM((nodes, nodes), jnp.bfloat16),
-            pltpu.SemaphoreType.DMA((4,)),
-        ),
-        params=PREP_PARAMS,
+        (first_leaf,) + tuple(far(a) for a in small_args + large_args),
+        (shaped((nodes, nodes), jnp.bfloat16), full, full, shaped((1, nodes)), small),
+        in_specs=[SMEM] + [HBM] * 9,
+        scratch=tuple(pltpu.VMEM(a.shape, a.dtype) for a in small_args + large_args)
+        + (pltpu.SemaphoreType.DMA((9,)),),
         name="prep",
     )
-    got = gather_parts(sums)
     for sweep in range(PROX_ITERS - 1):
         sums, z = call(
             lambda *refs: step_kernel(total_nodes, *refs),
@@ -317,10 +354,9 @@
         )
         got = gather_parts(sums)
     x, own, sent = call(
-        lambda *refs: last_kernel(total_nodes, *refs),
-        (leaf_weight, got, z, thin),
+        lambda *refs: last_kernel(total_nodes, leaves, *refs),
+        (got, z, thin),
         (full, full, shaped((groups, 16, LANES))),
-        in_specs=[SMEM] + [VMEM] * 3,
         scratch=(edge, edge),
         name="last_step",
     )

time: 154 us -> 146 us (0.948)
  blocking collectives: 137 us -> 123 us
  starting transfers between devices: 0 us -> 7.33 us
  waiting for transfers between devices: 0 us -> 5.46 us
  local copies, waits for them, and re-layouts: 5.38 us -> 0.08 us
    all_to_all x8 -> x7, blocking collectives: 90.7 us -> 76.1 us  [gather_parts(): return lax.all_to_all(spread, 'feeder', 0, 0)]
    all_to_all x0 -> x1, starting transfers between devices: none -> 7.33 us  [local(): got = lax.all_to_all(spread, 'feeder', 0, 0)]
    all_to_all x0 -> x1, waiting for transfers between devices: none -> 5.46 us  [local(): got = lax.all_to_all(spread, 'feeder', 0, 0)]
    unnamed x14 -> x2, local copies, waits for them, and re-layouts: 4.62 us -> 0.01 us
    pallas_call x11 -> x12, Pallas kernels: 9.77 us -> 9.18 us  [call(): pl.pallas_call(kernel, out_shape=outputs, in_specs=in_specs or [VMEM] * l...]
  transfers between devices with their start and end apart: 0 -> 1, of which waited for: 0 -> 1; matrix products, arithmetic and copies ran while one was open for 0% -> 0% of each run, Pallas kernels for 0% -> 1%
where the time goes in v5:
time: 146 us
  blocking collectives  123 us (84%)
  Pallas kernels  9.18 us (6%)
  starting transfers between devices  7.33 us (5%)
  waiting for transfers between devices  5.46 us (4%)
    all_to_all x7, blocking collectives, gather_parts(): return lax.all_to_all(spread, 'feeder', 0, 0)  76.1 us
    all_to_all x1, blocking collectives, local(): got = lax.all_to_all(sent, 'scen', 0, 0)  28.9 us
    all_to_all x1, blocking collectives, local(): got = lax.all_to_all(back, 'scen', 0, 0)  17.8 us
    pallas_call x12, Pallas kernels, call(): pl.pallas_call(kernel, out_shape=outputs, in_specs=in_specs or [VMEM] * l...  9.18 us
    all_to_all x1, starting transfers between devices, local(): got = lax.all_to_all(spread, 'feeder', 0, 0)  7.33 us
    all_to_all x1, waiting for transfers between devices, local(): got = lax.all_to_all(spread, 'feeder', 0, 0)  5.46 us
  transfers between devices with their start and end apart: 1, of which 1 were waited for; matrix products, arithmetic and copies ran while one was open for 0% of the time, Pallas kernels for 1%

profile of v5, /device:TPU:32, one launch (start us, length us, event | category | flops | bytes accessed | tf_op | source)
XLA Modules:
  0.0 145.7 jit_solution(9169724707392243899)
XLA Ops:
  0.6 1.9 %start_sums.1 = f32[32,3,128]{2,1,0:T(4,128)} custom-call(bf16[384,512]{1,0:T(8,128)(2,1)} %bitcast.13), custom_call_target="tpu_custom_call" | custom-call | tf_op jit(solution)/shard_map/start_sums/pallas_call | solution.py:287
  2.6 7.3 %all-to-all-start = ((f32[32,3,128]{2,1,0:T(4,128)}), f32[32,3,128]{2,1,0:T(4,128)S(1)}, u32[]{:S(2)}, u32[]{:S(2)}) async-start(f32[32,3,128]{2,1,0:T(4,128)} %start_sums.1), calls=%async_computation | async-start | bytes 131072 | tf_op jit(solution)/shard_map/all_to_all | solution.py:331
  9.9 2.1 %prep.1 = (bf16[512,512]{1,0:T(8,128)(2,1)S(1)}, f32[384,512]{1,0:T(8,128)S(1)}, f32[384,512]{1,0:T(8,128)S(1)}, f32[1,512]{1,0:T(1,128)S(1)}, f32[1568,128]{1,0:T(8,128)S(1)}) custom-call(s32[1]{0:T(128)} %bitcast.1.first_ref, f32[16,24]{1,0:T(8,128)} %target_hbm.1, s32[16,24]{1,0:T(8,128)} %bitcast.16, f32[1,16]{1,0:T(1,128)} %bitcast.19, ...), custom_call_target="tpu_custom_call" | custom-call | tf_op jit(solution)/shard_map/prep/pallas_call | solution.py:287
  12.0 5.5 %all-to-all-done.refs_0_ = f32[32,3,128]{2,1,0:T(4,128)S(1)} async-done(((f32[32,3,128]{2,1,0:T(4,128)}), f32[32,3,128]{2,1,0:T(4,128)S(1)}, u32[]{:S(2)}, u32[]{:S(2)}) %all-to-all-start) | async-done | bytes 49184 | tf_op jit(solution)/shard_map/all_to_all | solution.py:331
  17.4 0.5 prox_step.7
  17.9 10.9 %all_to_all.50.refs_0_ = f32[32,3,128]{2,1,0:T(4,128)S(1)} all-to-all(f32[32,3,128]{2,1,0:T(4,128)S(1)} %broadcast_in_dim.21), channel_id=1, replica_groups=mesh['feeder'=32,'scen'=16] {'feeder'}, dimensions={0} | all-to-all | bytes 98304 | tf_op jit(solution)/shard_map/all_to_all | solution.py:308
  28.8 0.5 prox_step.8
  29.3 10.9 %all_to_all.51.refs_0_ = f32[32,3,128]{2,1,0:T(4,128)S(1)} all-to-all(f32[32,3,128]{2,1,0:T(4,128)S(1)} %broadcast_in_dim.22), channel_id=1, replica_groups=mesh['feeder'=32,'scen'=16] {'feeder'}, dimensions={0} | all-to-all | bytes 98304 | tf_op jit(solution)/shard_map/all_to_all | solution.py:308
  40.1 0.5 prox_step.9
  40.6 10.9 %all_to_all.52.refs_0_ = f32[32,3,128]{2,1,0:T(4,128)S(1)} all-to-all(f32[32,3,128]{2,1,0:T(4,128)S(1)} %broadcast_in_dim.23), channel_id=1, replica_groups=mesh['feeder'=32,'scen'=16] {'feeder'}, dimensions={0} | all-to-all | bytes 98304 | tf_op jit(solution)/shard_map/all_to_all | solution.py:308
  51.5 0.5 prox_step.10
  52.0 10.9 %all_to_all.53.refs_0_ = f32[32,3,128]{2,1,0:T(4,128)S(1)} all-to-all(f32[32,3,128]{2,1,0:T(4,128)S(1)} %broadcast_in_dim.24), channel_id=1, replica_groups=mesh['feeder'=32,'scen'=16] {'feeder'}, dimensions={0} | all-to-all | bytes 98304 | tf_op jit(solution)/shard_map/all_to_all | solution.py:308
  62.8 0.5 prox_step.11
  63.3 10.9 %all_to_all.54.refs_0_ = f32[32,3,128]{2,1,0:T(4,128)S(1)} all-to-all(f32[32,3,128]{2,1,0:T(4,128)S(1)} %broadcast_in_dim.25), channel_id=1, replica_groups=mesh['feeder'=32,'scen'=16] {'feeder'}, dimensions={0} | all-to-all | bytes 98304 | tf_op jit(solution)/shard_map/all_to_all | solution.py:308
  74.2 0.5 prox_step.12
  74.7 10.9 %all_to_all.55.refs_0_ = f32[32,3,128]{2,1,0:T(4,128)S(1)} all-to-all(f32[32,3,128]{2,1,0:T(4,128)S(1)} %broadcast_in_dim.26), channel_id=1, replica_groups=mesh['feeder'=32,'scen'=16] {'feeder'}, dimensions={0} | all-to-all | bytes 98304 | tf_op jit(solution)/shard_map/all_to_all | solution.py:308
  85.6 0.5 prox_step.13
  86.0 10.9 %all_to_all.56.refs_0_ = f32[32,3,128]{2,1,0:T(4,128)S(1)} all-to-all(f32[32,3,128]{2,1,0:T(4,128)S(1)} %broadcast_in_dim.27), channel_id=1, replica_groups=mesh['feeder'=32,'scen'=16] {'feeder'}, dimensions={0} | all-to-all | bytes 98304 | tf_op jit(solution)/shard_map/all_to_all | solution.py:308
  96.9 0.0 copy-start
  96.9 0.3 last_step.1
  97.3 28.9 %all_to_all.57.got_ref = f32[16,16,128]{2,1,0:T(8,128)S(1)} all-to-all(f32[16,16,128]{2,1,0:T(8,128)S(1)} %get-tuple-element.47), channel_id=1, replica_groups=mesh['feeder'=32,'scen'=16] {'scen'}, dimensions={0} | all-to-all | bytes 262144 | tf_op jit(solution)/shard_map/all_to_all | solution.py:364
  126.2 0.2 owner_chain.1
  126.4 17.8 %all_to_all.58.got_ref = f32[16,3,4,128]{3,2,1,0:T(4,128)S(1)} all-to-all(f32[16,3,4,128]{3,2,1,0:T(4,128)S(1)} %owner_chain.1), channel_id=1, replica_groups=mesh['feeder'=32,'scen'=16] {'scen'}, dimensions={0} | all-to-all | bytes 196608 | tf_op jit(solution)/shard_map/all_to_all | solution.py:366
  144.2 0.0 copy-done
  144.2 1.5 %finish.1 = (f32[384,512]{1,0:T(8,128)}, f32[384,512]{1,0:T(8,128)}, f32[384,512]{1,0:T(8,128)}) custom-call(f32[16,3,4,128]{3,2,1,0:T(4,128)S(1)} %all_to_all.58.got_ref, f32[384,512]{1,0:T(8,128)S(1)} %get-tuple-element.48.own_ref, f32[1568,128]{1,0:T(8,128)S(1)} %get-tuple-element.46.refs_2_.thin_ref, f32[384,512]{1,0:T(8,128)S(1)} %get-tuple-element.49.x_ref, ...), custom_call_target="tpu_custom_call" | custom-call | tf_op jit(solution)/shard_map/finish/pallas_call | solution.py:287
  (7 shorter events, 0.1 us)
Async XLA Ops:
  2.6 14.9 %all-to-all-start = ((f32[32,3,128]{2,1,0:T(4,128)}), f32[32,3,128]{2,1,0:T(4,128)S(1)}, u32[]{:S(2)}, u32[]{:S(2)}) async-start(f32[32,3,128]{2,1,0:T(4,128)} %start_sums.1), calls=%async_computation | async-start | bytes 131072 | tf_op jit(solution)/shard_map/all_to_all | solution.py:331
  96.9 47.3 %copy-start = (f32[16,24,512]{2,1,0:T(8,128)S(1)}, f32[16,24,512]{2,1,0:T(8,128)}, u32[]{:S(2)}) copy-start(f32[16,24,512]{2,1,0:T(8,128)} %param.11) | copy-start | bytes 2359300

commit v6 on v5

--- a/solution.py
+++ b/solution.py
@@ -34,14 +34,10 @@
     return copies
 
 
-def sum_kernel(anchor_hbm, spread_ref, anchor_ref, sems):
-    parts = [pl.ds(i * LANES, LANES) for i in range(anchor_ref.shape[0] // LANES)]
-    copies = fetch([(anchor_hbm.at[part, :], anchor_ref.at[part, :]) for part in parts], sems)
-    for i, part in enumerate(parts):
-        copies[i].wait()
-        total = row_sums(anchor_ref[part, :].astype(jnp.float32))
-        for feeder in range(spread_ref.shape[0]):
-            spread_ref[feeder, i : i + 1, :] = total
+def put_sums(sums_ref, x_ref):
+    for start in range(0, x_ref.shape[0], LANES):
+        block = x_ref[start : start + LANES, :].astype(jnp.float32)
+        sums_ref[start // LANES : start // LANES + 1, :] = row_sums(block)
 
 
 def affine(x, image, gain, fixed):
@@ -59,15 +55,15 @@
 def prep_kernel(
     first_ref, target_hbm, anc_hbm, weight_hbm, mask_hbm, diag_hbm,
     q_hbm, anchor_hbm, cost_hbm, dual_hbm,
-    q_out, fixed_out, z_out, gain_out, thin_out,
+    sums_ref, q_out, fixed_out, z_out, gain_out, thin_out,
     target_ref, anc_ref, weight_ref, mask_ref, diag_ref,
     q_ref, anchor_ref, cost_ref, dual_ref, sems,
 ):
     sources = (
-        anc_hbm, weight_hbm, mask_hbm, diag_hbm, target_hbm, q_hbm, anchor_hbm, cost_hbm, dual_hbm
+        anc_hbm, weight_hbm, mask_hbm, diag_hbm, target_hbm, anchor_hbm, q_hbm, cost_hbm, dual_hbm
     )
     places = (
-        anc_ref, weight_ref, mask_ref, diag_ref, target_ref, q_ref, anchor_ref, cost_ref, dual_ref
+        anc_ref, weight_ref, mask_ref, diag_ref, target_ref, anchor_ref, q_ref, cost_ref, dual_ref
     )
     copies = fetch(list(zip(sources, places)), sems)
     copies[0].wait()
@@ -121,12 +117,13 @@
     width = q_ref.shape[0] // count
     keep = mask_ref[...].astype(jnp.float32)
     copies[5].wait()
+    put_sums(sums_ref, anchor_ref)
+    copies[6].wait()
     for i in range(count):
         for j in range(count):
             rows, cols = slice(i * width, (i + 1) * width), slice(j * width, (j + 1) * width)
             block = jnp.broadcast_to(keep[i : i + 1, j : j + 1], (width, width))
             q_out[rows, cols] = q_ref[rows, cols] * block.astype(jnp.bfloat16)
-    copies[6].wait()
     image = jnp.dot(anchor_ref[...], q_out[...], preferred_element_type=jnp.float32)
     z_out[...] = image
     copies[7].wait()
@@ -155,8 +152,7 @@
     total_nodes, got_ref, z_ref, q_ref, fixed_ref, gain_ref, sums_ref, z_out, x_ref
 ):
     clipped(total_nodes, got_ref, z_ref, x_ref)
-    for i in range(x_ref.shape[0] // LANES):
-        sums_ref[i : i + 1, :] = row_sums(x_ref[i * LANES : (i + 1) * LANES, :])
+    put_sums(sums_ref, x_ref)
     x = x_ref[...]
     image = jnp.dot(x.astype(jnp.bfloat16), q_ref[...], preferred_element_type=jnp.float32)
     z_out[...] = affine(x, image, gain_ref[...], fixed_ref[...])
@@ -319,31 +315,22 @@
     buffer = pltpu.VMEM((rows, nodes), jnp.float32)
     edge = pltpu.VMEM((sections, nodes), jnp.float32)
 
-    narrow = pltpu.VMEM((rows, nodes), jnp.bfloat16)
-    spread = call(
-        sum_kernel,
-        (far(flat(anchor)),),
-        shaped((lax.axis_size("feeder"),) + sums_shape.shape),
-        in_specs=[HBM],
-        scratch=(narrow, pltpu.SemaphoreType.DMA((rows // LANES,))),
-        name="start_sums",
-    )
-    got = lax.all_to_all(spread, "feeder", 0, 0)
     first_leaf = (lax.axis_index("scen") * leaves).astype(jnp.int32).reshape(1)
     small_args = (
         target, ancestor.T, leaf_weight.reshape(1, leaves), block_mask[0],
         diag_gain.reshape(1, nodes),
     )
     large_args = (q_mat, flat(anchor), flat(cost_lin), flat(dual))
-    q_eff, fixed, z, gain, thin = call(
+    sums, q_eff, fixed, z, gain, thin = call(
         prep_kernel,
         (first_leaf,) + tuple(far(a) for a in small_args + large_args),
-        (shaped((nodes, nodes), jnp.bfloat16), full, full, shaped((1, nodes)), small),
+        (sums_shape, shaped((nodes, nodes), jnp.bfloat16), full, full, shaped((1, nodes)), small),
         in_specs=[SMEM] + [HBM] * 9,
         scratch=tuple(pltpu.VMEM(a.shape, a.dtype) for a in small_args + large_args)
         + (pltpu.SemaphoreType.DMA((9,)),),
         name="prep",
     )
+    got = gather_parts(sums)
     for sweep in range(PROX_ITERS - 1):
         sums, z = call(
             lambda *refs: step_kernel(total_nodes, *refs),

time: 146 us -> 146 us (level)
  blocking collectives: 123 us -> 137 us
  starting transfers between devices: 7.33 us -> 0 us
  waiting for transfers between devices: 5.46 us -> 0 us
  Pallas kernels: 9.18 us -> 7.53 us
    all_to_all x7 -> x8, blocking collectives: 76.1 us -> 90.7 us  [gather_parts(): return lax.all_to_all(spread, 'feeder', 0, 0)]
    all_to_all x1 -> x0, starting transfers between devices: 7.33 us -> none  [local(): got = lax.all_to_all(spread, 'feeder', 0, 0)]
    all_to_all x1 -> x0, waiting for transfers between devices: 5.46 us -> none  [local(): got = lax.all_to_all(spread, 'feeder', 0, 0)]
    pallas_call x12 -> x11, Pallas kernels: 9.18 us -> 7.53 us  [call(): pl.pallas_call(kernel, out_shape=outputs, in_specs=in_specs or [VMEM] * l...]
  transfers between devices with their start and end apart: 1 -> 0, of which waited for: 1 -> 0; matrix products, arithmetic and copies ran while one was open for 0% -> 0% of each run, Pallas kernels for 1% -> 0%
where the time goes in v6:
time: 146 us
  blocking collectives  137 us (94%)
  Pallas kernels  7.53 us (5%)
    all_to_all x8, blocking collectives, gather_parts(): return lax.all_to_all(spread, 'feeder', 0, 0)  90.7 us
    all_to_all x1, blocking collectives, local(): got = lax.all_to_all(sent, 'scen', 0, 0)  28.9 us
    all_to_all x1, blocking collectives, local(): got = lax.all_to_all(back, 'scen', 0, 0)  17.8 us
    pallas_call x11, Pallas kernels, call(): pl.pallas_call(kernel, out_shape=outputs, in_specs=in_specs or [VMEM] * l...  7.53 us

profile of v6, /device:TPU:32, one launch (start us, length us, event | category | flops | bytes accessed | tf_op | source)
XLA Modules:
  0.0 145.9 jit_solution(1714705082924806315)
XLA Ops:
  0.6 2.2 %prep.1 = (f32[3,128]{1,0:T(4,128)S(1)}, bf16[512,512]{1,0:T(8,128)(2,1)S(1)}, f32[384,512]{1,0:T(8,128)S(1)}, f32[384,512]{1,0:T(8,128)S(1)}, f32[1,512]{1,0:T(1,128)S(1)}, /*index=5*/f32[1568,128]{1,0:T(8,128)S(1)}) custom-call(s32[1]{0:T(128)} %bitcast.first_ref, f32[16,24]{1,0:T(8,128)} %target_hbm.1, s32[16,24]{1,0:T(8,128)} %bitcast.15, ...), custom_call_target="tpu_custom_call" | custom-call | tf_op jit(solution)/shard_map/prep/pallas_call | solution.py:283
  2.8 14.6 %all_to_all.50.refs_0_ = f32[32,3,128]{2,1,0:T(4,128)S(1)} all-to-all(f32[32,3,128]{2,1,0:T(4,128)S(1)} %broadcast_in_dim.24), channel_id=1, replica_groups=mesh['feeder'=32,'scen'=16] {'feeder'}, dimensions={0} | all-to-all | bytes 98304 | tf_op jit(solution)/shard_map/all_to_all | solution.py:304
  17.5 0.5 prox_step.7
  18.0 10.9 %all_to_all.51.refs_0_ = f32[32,3,128]{2,1,0:T(4,128)S(1)} all-to-all(f32[32,3,128]{2,1,0:T(4,128)S(1)} %broadcast_in_dim.25), channel_id=1, replica_groups=mesh['feeder'=32,'scen'=16] {'feeder'}, dimensions={0} | all-to-all | bytes 98304 | tf_op jit(solution)/shard_map/all_to_all | solution.py:304
  28.8 0.5 prox_step.8
  29.4 10.9 %all_to_all.52.refs_0_ = f32[32,3,128]{2,1,0:T(4,128)S(1)} all-to-all(f32[32,3,128]{2,1,0:T(4,128)S(1)} %broadcast_in_dim.26), channel_id=1, replica_groups=mesh['feeder'=32,'scen'=16] {'feeder'}, dimensions={0} | all-to-all | bytes 98304 | tf_op jit(solution)/shard_map/all_to_all | solution.py:304
  40.2 0.5 prox_step.9
  40.7 10.9 %all_to_all.53.refs_0_ = f32[32,3,128]{2,1,0:T(4,128)S(1)} all-to-all(f32[32,3,128]{2,1,0:T(4,128)S(1)} %broadcast_in_dim.27), channel_id=1, replica_groups=mesh['feeder'=32,'scen'=16] {'feeder'}, dimensions={0} | all-to-all | bytes 98304 | tf_op jit(solution)/shard_map/all_to_all | solution.py:304
  51.6 0.5 prox_step.10
  52.1 10.9 %all_to_all.54.refs_0_ = f32[32,3,128]{2,1,0:T(4,128)S(1)} all-to-all(f32[32,3,128]{2,1,0:T(4,128)S(1)} %broadcast_in_dim.28), channel_id=1, replica_groups=mesh['feeder'=32,'scen'=16] {'feeder'}, dimensions={0} | all-to-all | bytes 98304 | tf_op jit(solution)/shard_map/all_to_all | solution.py:304
  63.0 0.5 prox_step.11
  63.5 10.9 %all_to_all.55.refs_0_ = f32[32,3,128]{2,1,0:T(4,128)S(1)} all-to-all(f32[32,3,128]{2,1,0:T(4,128)S(1)} %broadcast_in_dim.29), channel_id=1, replica_groups=mesh['feeder'=32,'scen'=16] {'feeder'}, dimensions={0} | all-to-all | bytes 98304 | tf_op jit(solution)/shard_map/all_to_all | solution.py:304
  74.4 0.5 prox_step.12
  74.9 10.9 %all_to_all.56.refs_0_ = f32[32,3,128]{2,1,0:T(4,128)S(1)} all-to-all(f32[32,3,128]{2,1,0:T(4,128)S(1)} %broadcast_in_dim.30), channel_id=1, replica_groups=mesh['feeder'=32,'scen'=16] {'feeder'}, dimensions={0} | all-to-all | bytes 98304 | tf_op jit(solution)/shard_map/all_to_all | solution.py:304
  85.7 0.5 prox_step.13
  86.2 10.9 %all_to_all.57.refs_0_ = f32[32,3,128]{2,1,0:T(4,128)S(1)} all-to-all(f32[32,3,128]{2,1,0:T(4,128)S(1)} %broadcast_in_dim.31), channel_id=1, replica_groups=mesh['feeder'=32,'scen'=16] {'feeder'}, dimensions={0} | all-to-all | bytes 98304 | tf_op jit(solution)/shard_map/all_to_all | solution.py:304
  97.1 0.0 copy-start
  97.1 0.3 last_step.1
  97.5 28.9 %all_to_all.58.got_ref = f32[16,16,128]{2,1,0:T(8,128)S(1)} all-to-all(f32[16,16,128]{2,1,0:T(8,128)S(1)} %get-tuple-element.49), channel_id=1, replica_groups=mesh['feeder'=32,'scen'=16] {'scen'}, dimensions={0} | all-to-all | bytes 262144 | tf_op jit(solution)/shard_map/all_to_all | solution.py:351
  126.4 0.2 owner_chain.1
  126.6 17.8 %all_to_all.59.got_ref = f32[16,3,4,128]{3,2,1,0:T(4,128)S(1)} all-to-all(f32[16,3,4,128]{3,2,1,0:T(4,128)S(1)} %owner_chain.1), channel_id=1, replica_groups=mesh['feeder'=32,'scen'=16] {'scen'}, dimensions={0} | all-to-all | bytes 196608 | tf_op jit(solution)/shard_map/all_to_all | solution.py:353
  144.4 0.0 copy-done
  144.4 1.5 %finish.1 = (f32[384,512]{1,0:T(8,128)}, f32[384,512]{1,0:T(8,128)}, f32[384,512]{1,0:T(8,128)}) custom-call(f32[16,3,4,128]{3,2,1,0:T(4,128)S(1)} %all_to_all.59.got_ref, f32[384,512]{1,0:T(8,128)S(1)} %get-tuple-element.50.own_ref, f32[1568,128]{1,0:T(8,128)S(1)} %get-tuple-element.48.refs_2_.thin_ref, f32[384,512]{1,0:T(8,128)S(1)} %get-tuple-element.51.x_ref, ...), custom_call_target="tpu_custom_call" | custom-call | tf_op jit(solution)/shard_map/finish/pallas_call | solution.py:283
  (8 shorter events, 0.1 us)
Async XLA Ops:
  97.1 47.2 %copy-start = (f32[16,24,512]{2,1,0:T(8,128)S(1)}, f32[16,24,512]{2,1,0:T(8,128)}, u32[]{:S(2)}) copy-start(f32[16,24,512]{2,1,0:T(8,128)} %param.11) | copy-start | bytes 2359300

commit v7 on v5

--- a/solution.py
+++ b/solution.py
@@ -191,29 +191,34 @@
             recip = slice(rows_all + i * sections, rows_all + (i + 1) * sections)
             own_ref[rows, cols] = total * thin_ref[recip, :]
         head_ref[:, cols] = total * thin_ref[end : end + sections, :]
-    zeros = jnp.zeros((8 - per, LANES), jnp.float32)
     for owner in range(owners):
         block, col = owner // node_blocks, owner % node_blocks
-        rows, cols = slice(block * per, (block + 1) * per), slice(col * LANES, (col + 1) * LANES)
+        cols = slice(col * LANES, (col + 1) * LANES)
         spot = end + sections + block
-        sent_ref[owner, 0:per, :] = tail_ref[rows, cols]
-        sent_ref[owner, per:8, :] = zeros
-        sent_ref[owner, per : per + 1, :] = thin_ref[spot : spot + 1, :]
-        sent_ref[owner, 8 : 8 + per, :] = head_ref[rows, cols]
-        sent_ref[owner, 8 + per : 16, :] = zeros
-
-
-def owner_kernel(got_ref, back_ref):
+        lines = [(ref, block * per + j, cols) for ref in (tail_ref, head_ref) for j in range(per)]
+        for j, (ref, row, part) in enumerate(lines + [(thin_ref, spot, slice(0, LANES))]):
+            sent_ref[owner, :, j * LANES : (j + 1) * LANES] = ref[row : row + 1, part]
+
+
+def owner_kernel(got_ref, back_ref, tile_ref):
     per = back_ref.shape[1] * back_ref.shape[2] // 2
     groups = got_ref.shape[0]
     shape = (8, LANES)
-    tails = [got_ref[g, 0:8, :] for g in range(groups)]
-    heads = [got_ref[g, 8:16, :] for g in range(groups)]
+    for g in range(groups):
+        for j in range(2 * per):
+            spot = j if j < per else 8 + j - per
+            tile_ref[g, spot : spot + 1, :] = got_ref[g, :, j * LANES : (j + 1) * LANES]
+    zeros = jnp.zeros((8 - per, LANES), jnp.float32)
+    for g in range(groups):
+        tile_ref[g, per:8, :] = zeros
+        tile_ref[g, 8 + per : 16, :] = zeros
+    tails = [tile_ref[g, 0:8, :] for g in range(groups)]
+    heads = [tile_ref[g, 8:16, :] for g in range(groups)]
     down = lax.broadcasted_iota(jnp.int32, shape, 0)
     across = lax.broadcasted_iota(jnp.int32, shape, 1)
 
     def scalars(g, first):
-        line = jnp.broadcast_to(got_ref[g, per : per + 1, :], shape)
+        line = jnp.broadcast_to(got_ref[g, :, 2 * per * LANES :], shape)
         mine = jnp.where(across == down + first, line, 0.0)
         return jnp.broadcast_to(jnp.sum(mine, axis=1, keepdims=True), shape)
 
@@ -353,16 +358,17 @@
             name="prox_step",
         )
         got = gather_parts(sums)
+    per = sections * (nodes // LANES) // groups
     x, own, sent = call(
         lambda *refs: last_kernel(total_nodes, leaves, *refs),
         (got, z, thin),
-        (full, full, shaped((groups, 16, LANES))),
+        (full, full, shaped((groups, 1, (2 * per + 1) * LANES))),
         scratch=(edge, edge),
         name="last_step",
     )
-    per = sections * (nodes // LANES) // groups
     got = lax.all_to_all(sent, "scen", 0, 0)
-    back = call(owner_kernel, (got,), shaped((groups, per // 2, 4, LANES)), name="owner_chain")
+    back = call(owner_kernel, (got,), shaped((groups, per // 2, 4, LANES)),
+                scratch=(pltpu.VMEM((groups, 16, LANES), jnp.float32),), name="owner_chain")
     got = lax.all_to_all(back, "scen", 0, 0)
     x, average, new_dual = call(
         final_kernel,

time: 146 us -> 145 us (level)
  blocking collectives: 123 us -> 121 us
where the time goes in v7:
time: 145 us; the launch traced here: 144 us
  blocking collectives  121 us (83%)
  Pallas kernels  9.22 us (6%)
  starting transfers between devices  7.33 us (5%)
  waiting for transfers between devices  5.46 us (4%)
    all_to_all x7, blocking collectives, gather_parts(): return lax.all_to_all(spread, 'feeder', 0, 0)  76.1 us
    all_to_all x1, blocking collectives, local(): got = lax.all_to_all(sent, 'scen', 0, 0)  28.5 us
    all_to_all x1, blocking collectives, local(): got = lax.all_to_all(back, 'scen', 0, 0)  16.7 us
    pallas_call x12, Pallas kernels, call(): pl.pallas_call(kernel, out_shape=outputs, in_specs=in_specs or [VMEM] * l...  9.22 us
    all_to_all x1, starting transfers between devices, local(): got = lax.all_to_all(spread, 'feeder', 0, 0)  7.33 us
    all_to_all x1, waiting for transfers between devices, local(): got = lax.all_to_all(spread, 'feeder', 0, 0)  5.46 us
  transfers between devices with their start and end apart: 1, of which 1 were waited for; matrix products, arithmetic and copies ran while one was open for 0% of the time, Pallas kernels for 1%

profile of v7, /device:TPU:32, one launch (start us, length us, event | category | flops | bytes accessed | tf_op | source)
XLA Modules:
  0.0 144.2 jit_solution(16617463925203294654)
XLA Ops:
  0.6 1.9 %start_sums.1 = f32[32,3,128]{2,1,0:T(4,128)} custom-call(bf16[384,512]{1,0:T(8,128)(2,1)} %bitcast.13), custom_call_target="tpu_custom_call" | custom-call | tf_op jit(solution)/shard_map/start_sums/pallas_call | solution.py:292
  2.6 7.3 %all-to-all-start = ((f32[32,3,128]{2,1,0:T(4,128)}), f32[32,3,128]{2,1,0:T(4,128)S(1)}, u32[]{:S(2)}, u32[]{:S(2)}) async-start(f32[32,3,128]{2,1,0:T(4,128)} %start_sums.1), calls=%async_computation | async-start | bytes 131072 | tf_op jit(solution)/shard_map/all_to_all | solution.py:336
  9.9 2.1 %prep.1 = (bf16[512,512]{1,0:T(8,128)(2,1)S(1)}, f32[384,512]{1,0:T(8,128)S(1)}, f32[384,512]{1,0:T(8,128)S(1)}, f32[1,512]{1,0:T(1,128)S(1)}, f32[1568,128]{1,0:T(8,128)S(1)}) custom-call(s32[1]{0:T(128)} %bitcast.1.first_ref, f32[16,24]{1,0:T(8,128)} %target_hbm.1, s32[16,24]{1,0:T(8,128)} %bitcast.16, f32[1,16]{1,0:T(1,128)} %bitcast.19, ...), custom_call_target="tpu_custom_call" | custom-call | tf_op jit(solution)/shard_map/prep/pallas_call | solution.py:292
  12.0 5.5 %all-to-all-done.refs_0_ = f32[32,3,128]{2,1,0:T(4,128)S(1)} async-done(((f32[32,3,128]{2,1,0:T(4,128)}), f32[32,3,128]{2,1,0:T(4,128)S(1)}, u32[]{:S(2)}, u32[]{:S(2)}) %all-to-all-start) | async-done | bytes 49184 | tf_op jit(solution)/shard_map/all_to_all | solution.py:336
  17.4 0.5 prox_step.7
  17.9 10.9 %all_to_all.50.refs_0_ = f32[32,3,128]{2,1,0:T(4,128)S(1)} all-to-all(f32[32,3,128]{2,1,0:T(4,128)S(1)} %broadcast_in_dim.21), channel_id=1, replica_groups=mesh['feeder'=32,'scen'=16] {'feeder'}, dimensions={0} | all-to-all | bytes 98304 | tf_op jit(solution)/shard_map/all_to_all | solution.py:313
  28.8 0.5 prox_step.8
  29.3 10.9 %all_to_all.51.refs_0_ = f32[32,3,128]{2,1,0:T(4,128)S(1)} all-to-all(f32[32,3,128]{2,1,0:T(4,128)S(1)} %broadcast_in_dim.22), channel_id=1, replica_groups=mesh['feeder'=32,'scen'=16] {'feeder'}, dimensions={0} | all-to-all | bytes 98304 | tf_op jit(solution)/shard_map/all_to_all | solution.py:313
  40.1 0.5 prox_step.9
  40.6 10.9 %all_to_all.52.refs_0_ = f32[32,3,128]{2,1,0:T(4,128)S(1)} all-to-all(f32[32,3,128]{2,1,0:T(4,128)S(1)} %broadcast_in_dim.23), channel_id=1, replica_groups=mesh['feeder'=32,'scen'=16] {'feeder'}, dimensions={0} | all-to-all | bytes 98304 | tf_op jit(solution)/shard_map/all_to_all | solution.py:313
  51.5 0.5 prox_step.10
  52.0 10.9 %all_to_all.53.refs_0_ = f32[32,3,128]{2,1,0:T(4,128)S(1)} all-to-all(f32[32,3,128]{2,1,0:T(4,128)S(1)} %broadcast_in_dim.24), channel_id=1, replica_groups=mesh['feeder'=32,'scen'=16] {'feeder'}, dimensions={0} | all-to-all | bytes 98304 | tf_op jit(solution)/shard_map/all_to_all | solution.py:313
  62.8 0.5 prox_step.11
  63.3 10.9 %all_to_all.54.refs_0_ = f32[32,3,128]{2,1,0:T(4,128)S(1)} all-to-all(f32[32,3,128]{2,1,0:T(4,128)S(1)} %broadcast_in_dim.25), channel_id=1, replica_groups=mesh['feeder'=32,'scen'=16] {'feeder'}, dimensions={0} | all-to-all | bytes 98304 | tf_op jit(solution)/shard_map/all_to_all | solution.py:313
  74.2 0.5 prox_step.12
  74.7 10.9 %all_to_all.55.refs_0_ = f32[32,3,128]{2,1,0:T(4,128)S(1)} all-to-all(f32[32,3,128]{2,1,0:T(4,128)S(1)} %broadcast_in_dim.26), channel_id=1, replica_groups=mesh['feeder'=32,'scen'=16] {'feeder'}, dimensions={0} | all-to-all | bytes 98304 | tf_op jit(solution)/shard_map/all_to_all | solution.py:313
  85.6 0.5 prox_step.13
  86.0 10.9 %all_to_all.56.refs_0_ = f32[32,3,128]{2,1,0:T(4,128)S(1)} all-to-all(f32[32,3,128]{2,1,0:T(4,128)S(1)} %broadcast_in_dim.27), channel_id=1, replica_groups=mesh['feeder'=32,'scen'=16] {'feeder'}, dimensions={0} | all-to-all | bytes 98304 | tf_op jit(solution)/shard_map/all_to_all | solution.py:313
  96.9 0.0 copy-start
  96.9 0.4 last_step.1
  97.3 28.5 %all_to_all.57.got_ref = f32[16,1,1664]{2,1,0:T(1,128)S(1)} all-to-all(f32[16,1,1664]{2,1,0:T(1,128)S(1)} %get-tuple-element.47), channel_id=1, replica_groups=mesh['feeder'=32,'scen'=16] {'scen'}, dimensions={0} | all-to-all | bytes 212992 | tf_op jit(solution)/shard_map/all_to_all | solution.py:369
  125.8 0.2 owner_chain.1
  126.0 16.7 %all_to_all.58.got_ref = f32[16,3,4,128]{3,2,1,0:T(4,128)S(1)} all-to-all(f32[16,3,4,128]{3,2,1,0:T(4,128)S(1)} %owner_chain.1), channel_id=1, replica_groups=mesh['feeder'=32,'scen'=16] {'scen'}, dimensions={0} | all-to-all | bytes 196608 | tf_op jit(solution)/shard_map/all_to_all | solution.py:372
  142.7 0.0 copy-done
  142.7 1.5 %finish.1 = (f32[384,512]{1,0:T(8,128)}, f32[384,512]{1,0:T(8,128)}, f32[384,512]{1,0:T(8,128)}) custom-call(f32[16,3,4,128]{3,2,1,0:T(4,128)S(1)} %all_to_all.58.got_ref, f32[384,512]{1,0:T(8,128)S(1)} %get-tuple-element.48.own_ref, f32[1568,128]{1,0:T(8,128)S(1)} %get-tuple-element.46.refs_2_.thin_ref, f32[384,512]{1,0:T(8,128)S(1)} %get-tuple-element.49.x_ref, ...), custom_call_target="tpu_custom_call" | custom-call | tf_op jit(solution)/shard_map/finish/pallas_call | solution.py:292
  (7 shorter events, 0.1 us)
Async XLA Ops:
  2.6 14.9 %all-to-all-start = ((f32[32,3,128]{2,1,0:T(4,128)}), f32[32,3,128]{2,1,0:T(4,128)S(1)}, u32[]{:S(2)}, u32[]{:S(2)}) async-start(f32[32,3,128]{2,1,0:T(4,128)} %start_sums.1), calls=%async_computation | async-start | bytes 131072 | tf_op jit(solution)/shard_map/all_to_all | solution.py:336
  96.9 45.8 %copy-start = (f32[16,24,512]{2,1,0:T(8,128)S(1)}, f32[16,24,512]{2,1,0:T(8,128)}, u32[]{:S(2)}) copy-start(f32[16,24,512]{2,1,0:T(8,128)} %param.11) | copy-start | bytes 2359300

commit v8 on v7

--- a/solution.py
+++ b/solution.py
@@ -34,14 +34,18 @@
     return copies
 
 
+def put_spread(spread_ref, i, line):
+    for feeder in range(spread_ref.shape[0]):
+        spread_ref[feeder, :, i * LANES : (i + 1) * LANES] = line
+
+
 def sum_kernel(anchor_hbm, spread_ref, anchor_ref, sems):
     parts = [pl.ds(i * LANES, LANES) for i in range(anchor_ref.shape[0] // LANES)]
     copies = fetch([(anchor_hbm.at[part, :], anchor_ref.at[part, :]) for part in parts], sems)
     for i, part in enumerate(parts):
         copies[i].wait()
         total = row_sums(anchor_ref[part, :].astype(jnp.float32))
-        for feeder in range(spread_ref.shape[0]):
-            spread_ref[feeder, i : i + 1, :] = total
+        put_spread(spread_ref, i, total)
 
 
 def affine(x, image, gain, fixed):
@@ -145,18 +149,18 @@
     shift = jnp.sum(got_ref[...], axis=0) * (step_size * coupling / total_nodes)
     for i in range(z_ref.shape[0] // LANES):
         rows = slice(i * LANES, (i + 1) * LANES)
-        tile = jnp.broadcast_to(shift[i : i + 1, :], (LANES, LANES)).T
+        tile = jnp.broadcast_to(shift[:, rows], (LANES, LANES)).T
         for start in range(0, z_ref.shape[1], LANES):
             cols = slice(start, start + LANES)
             x_ref[rows, cols] = jnp.clip(z_ref[rows, cols] - tile, -power_limit, power_limit)
 
 
 def step_kernel(
-    total_nodes, got_ref, z_ref, q_ref, fixed_ref, gain_ref, sums_ref, z_out, x_ref
+    total_nodes, got_ref, z_ref, q_ref, fixed_ref, gain_ref, spread_ref, z_out, x_ref
 ):
     clipped(total_nodes, got_ref, z_ref, x_ref)
     for i in range(x_ref.shape[0] // LANES):
-        sums_ref[i : i + 1, :] = row_sums(x_ref[i * LANES : (i + 1) * LANES, :])
+        put_spread(spread_ref, i, row_sums(x_ref[i * LANES : (i + 1) * LANES, :]))
     x = x_ref[...]
     image = jnp.dot(x.astype(jnp.bfloat16), q_ref[...], preferred_element_type=jnp.float32)
     z_out[...] = affine(x, image, gain_ref[...], fixed_ref[...])
@@ -308,18 +312,13 @@
     return pltpu.with_memory_space_constraint(array, pltpu.HBM)
 
 
-def gather_parts(part):
-    spread = jnp.broadcast_to(part, (lax.axis_size("feeder"),) + part.shape)
-    return lax.all_to_all(spread, "feeder", 0, 0)
-
-
 def local(anchor, cost_lin, dual, target, leaf_weight, q_mat, diag_gain, block_mask, ancestor):
     leaves, sections, nodes = anchor.shape
     rows = leaves * sections
     groups = lax.axis_size("scen")
     total_nodes = lax.axis_size("feeder") * nodes
     flat = lambda a: a.reshape(rows, nodes)
-    sums_shape = shaped((rows // LANES, LANES))
+    spread_shape = shaped((lax.axis_size("feeder"), 1, rows))
     full, small = shaped((rows, nodes)), shaped((4 * rows + sections + 8, LANES))
     buffer = pltpu.VMEM((rows, nodes), jnp.float32)
     edge = pltpu.VMEM((sections, nodes), jnp.float32)
@@ -328,7 +327,7 @@
     spread = call(
         sum_kernel,
         (far(flat(anchor)),),
-        shaped((lax.axis_size("feeder"),) + sums_shape.shape),
+        spread_shape,
         in_specs=[HBM],
         scratch=(narrow, pltpu.SemaphoreType.DMA((rows // LANES,))),
         name="start_sums",
@@ -350,14 +349,14 @@
         name="prep",
     )
     for sweep in range(PROX_ITERS - 1):
-        sums, z = call(
+        spread, z = call(
             lambda *refs: step_kernel(total_nodes, *refs),
             (got, z, q_eff, fixed, gain),
-            (sums_shape, full),
+            (spread_shape, full),
             scratch=(buffer,),
             name="prox_step",
         )
-        got = gather_parts(sums)
+        got = lax.all_to_all(spread, "feeder", 0, 0)
     per = sections * (nodes // LANES) // groups
     x, own, sent = call(
         lambda *refs: last_kernel(total_nodes, leaves, *refs),

time: 145 us -> 144 us (level)
  no operation moved by 1% of the time
where the time goes in v8:
time: 144 us
  blocking collectives  121 us (84%)
  Pallas kernels  9.3 us (6%)
  starting transfers between devices  7.33 us (5%)
  waiting for transfers between devices  5.41 us (4%)
    all_to_all x7, blocking collectives, local(): got = lax.all_to_all(spread, 'feeder', 0, 0)  75.7 us
    all_to_all x1, blocking collectives, local(): got = lax.all_to_all(sent, 'scen', 0, 0)  28.5 us
    all_to_all x1, blocking collectives, local(): got = lax.all_to_all(back, 'scen', 0, 0)  16.7 us
    pallas_call x12, Pallas kernels, call(): pl.pallas_call(kernel, out_shape=outputs, in_specs=in_specs or [VMEM] * l...  9.3 us
    all_to_all x1, starting transfers between devices, local(): got = lax.all_to_all(spread, 'feeder', 0, 0)  7.33 us
    all_to_all x1, waiting for transfers between devices, local(): got = lax.all_to_all(spread, 'feeder', 0, 0)  5.41 us
  transfers between devices with their start and end apart: 1, of which 1 were waited for; matrix products, arithmetic and copies ran while one was open for 0% of the time, Pallas kernels for 1%

profile of v8, /device:TPU:32, one launch (start us, length us, event | category | flops | bytes accessed | tf_op | source)
XLA Modules:
  0.0 143.7 jit_solution(11509068475480696252)
XLA Ops:
  0.6 1.9 %start_sums.1 = f32[32,1,384]{2,1,0:T(1,128)} custom-call(bf16[384,512]{1,0:T(8,128)(2,1)} %bitcast.13), custom_call_target="tpu_custom_call" | custom-call | tf_op jit(solution)/shard_map/start_sums/pallas_call | solution.py:296
  2.5 7.3 %all-to-all-start = ((f32[32,1,384]{2,1,0:T(1,128)}), f32[32,1,384]{2,1,0:T(1,128)S(1)}, u32[]{:S(2)}, u32[]{:S(2)}) async-start(f32[32,1,384]{2,1,0:T(1,128)} %start_sums.1), calls=%async_computation | async-start | bytes 98304 | tf_op jit(solution)/shard_map/all_to_all | solution.py:335
  9.9 2.1 %prep.1 = (bf16[512,512]{1,0:T(8,128)(2,1)S(1)}, f32[384,512]{1,0:T(8,128)S(1)}, f32[384,512]{1,0:T(8,128)S(1)}, f32[1,512]{1,0:T(1,128)S(1)}, f32[1568,128]{1,0:T(8,128)S(1)}) custom-call(s32[1]{0:T(128)} %bitcast.1.first_ref, f32[16,24]{1,0:T(8,128)} %target_hbm.1, s32[16,24]{1,0:T(8,128)} %bitcast.16, f32[1,16]{1,0:T(1,128)} %bitcast.19, ...), custom_call_target="tpu_custom_call" | custom-call | tf_op jit(solution)/shard_map/prep/pallas_call | solution.py:296
  12.0 5.4 %all-to-all-done.refs_0_ = f32[32,1,384]{2,1,0:T(1,128)S(1)} async-done(((f32[32,1,384]{2,1,0:T(1,128)}), f32[32,1,384]{2,1,0:T(1,128)S(1)}, u32[]{:S(2)}, u32[]{:S(2)}) %all-to-all-start) | async-done | bytes 49184 | tf_op jit(solution)/shard_map/all_to_all | solution.py:335
  17.4 0.5 prox_step.7
  17.8 10.8 %all_to_all.50.refs_0_ = f32[32,1,384]{2,1,0:T(1,128)S(1)} all-to-all(f32[32,1,384]{2,1,0:T(1,128)S(1)} %get-tuple-element.32), channel_id=1, replica_groups=mesh['feeder'=32,'scen'=16] {'feeder'}, dimensions={0} | all-to-all | bytes 98304 | tf_op jit(solution)/shard_map/all_to_all | solution.py:359
  28.7 0.5 prox_step.8
  29.1 10.8 %all_to_all.51.refs_0_ = f32[32,1,384]{2,1,0:T(1,128)S(1)} all-to-all(f32[32,1,384]{2,1,0:T(1,128)S(1)} %get-tuple-element.34), channel_id=1, replica_groups=mesh['feeder'=32,'scen'=16] {'feeder'}, dimensions={0} | all-to-all | bytes 98304 | tf_op jit(solution)/shard_map/all_to_all | solution.py:359
  39.9 0.5 prox_step.9
  40.4 10.8 %all_to_all.52.refs_0_ = f32[32,1,384]{2,1,0:T(1,128)S(1)} all-to-all(f32[32,1,384]{2,1,0:T(1,128)S(1)} %get-tuple-element.36), channel_id=1, replica_groups=mesh['feeder'=32,'scen'=16] {'feeder'}, dimensions={0} | all-to-all | bytes 98304 | tf_op jit(solution)/shard_map/all_to_all | solution.py:359
  51.2 0.5 prox_step.10
  51.7 10.8 %all_to_all.53.refs_0_ = f32[32,1,384]{2,1,0:T(1,128)S(1)} all-to-all(f32[32,1,384]{2,1,0:T(1,128)S(1)} %get-tuple-element.38), channel_id=1, replica_groups=mesh['feeder'=32,'scen'=16] {'feeder'}, dimensions={0} | all-to-all | bytes 98304 | tf_op jit(solution)/shard_map/all_to_all | solution.py:359
  62.5 0.5 prox_step.11
  63.0 10.8 %all_to_all.54.refs_0_ = f32[32,1,384]{2,1,0:T(1,128)S(1)} all-to-all(f32[32,1,384]{2,1,0:T(1,128)S(1)} %get-tuple-element.40), channel_id=1, replica_groups=mesh['feeder'=32,'scen'=16] {'feeder'}, dimensions={0} | all-to-all | bytes 98304 | tf_op jit(solution)/shard_map/all_to_all | solution.py:359
  73.8 0.5 prox_step.12
  74.3 10.8 %all_to_all.55.refs_0_ = f32[32,1,384]{2,1,0:T(1,128)S(1)} all-to-all(f32[32,1,384]{2,1,0:T(1,128)S(1)} %get-tuple-element.42), channel_id=1, replica_groups=mesh['feeder'=32,'scen'=16] {'feeder'}, dimensions={0} | all-to-all | bytes 98304 | tf_op jit(solution)/shard_map/all_to_all | solution.py:359
  85.1 0.5 prox_step.13
  85.6 10.8 %all_to_all.56.refs_0_ = f32[32,1,384]{2,1,0:T(1,128)S(1)} all-to-all(f32[32,1,384]{2,1,0:T(1,128)S(1)} %get-tuple-element.44), channel_id=1, replica_groups=mesh['feeder'=32,'scen'=16] {'feeder'}, dimensions={0} | all-to-all | bytes 98304 | tf_op jit(solution)/shard_map/all_to_all | solution.py:359
  96.4 0.0 copy-start
  96.4 0.4 last_step.1
  96.8 28.5 %all_to_all.57.got_ref = f32[16,1,1664]{2,1,0:T(1,128)S(1)} all-to-all(f32[16,1,1664]{2,1,0:T(1,128)S(1)} %get-tuple-element.47), channel_id=1, replica_groups=mesh['feeder'=32,'scen'=16] {'scen'}, dimensions={0} | all-to-all | bytes 212992 | tf_op jit(solution)/shard_map/all_to_all | solution.py:368
  125.3 0.2 owner_chain.1
  125.5 16.7 %all_to_all.58.got_ref = f32[16,3,4,128]{3,2,1,0:T(4,128)S(1)} all-to-all(f32[16,3,4,128]{3,2,1,0:T(4,128)S(1)} %owner_chain.1), channel_id=1, replica_groups=mesh['feeder'=32,'scen'=16] {'scen'}, dimensions={0} | all-to-all | bytes 196608 | tf_op jit(solution)/shard_map/all_to_all | solution.py:371
  142.2 0.0 copy-done
  142.2 1.5 %finish.1 = (f32[384,512]{1,0:T(8,128)}, f32[384,512]{1,0:T(8,128)}, f32[384,512]{1,0:T(8,128)}) custom-call(f32[16,3,4,128]{3,2,1,0:T(4,128)S(1)} %all_to_all.58.got_ref, f32[384,512]{1,0:T(8,128)S(1)} %get-tuple-element.48.own_ref, f32[1568,128]{1,0:T(8,128)S(1)} %get-tuple-element.46.refs_2_.thin_ref, f32[384,512]{1,0:T(8,128)S(1)} %get-tuple-element.49.x_ref, ...), custom_call_target="tpu_custom_call" | custom-call | tf_op jit(solution)/shard_map/finish/pallas_call | solution.py:296
Async XLA Ops:
  2.5 14.8 %all-to-all-start = ((f32[32,1,384]{2,1,0:T(1,128)}), f32[32,1,384]{2,1,0:T(1,128)S(1)}, u32[]{:S(2)}, u32[]{:S(2)}) async-start(f32[32,1,384]{2,1,0:T(1,128)} %start_sums.1), calls=%async_computation | async-start | bytes 98304 | tf_op jit(solution)/shard_map/all_to_all | solution.py:335
  96.4 45.8 %copy-start = (f32[16,24,512]{2,1,0:T(8,128)S(1)}, f32[16,24,512]{2,1,0:T(8,128)}, u32[]{:S(2)}) copy-start(f32[16,24,512]{2,1,0:T(8,128)} %param.11) | copy-start | bytes 2359300

commit v9 on v7

--- a/solution.py
+++ b/solution.py
@@ -376,7 +376,7 @@
         (full, full, full),
         out_specs=(HBM, HBM, HBM),
         scratch=(
-            edge, edge, buffer, buffer, pltpu.SemaphoreType.DMA((2, 4)), pltpu.SemaphoreType.DMA
+            edge, edge, buffer, buffer, pltpu.SemaphoreType.DMA((2, 8)), pltpu.SemaphoreType.DMA
         ),
         name="finish",
     )

time: 145 us -> 145 us (level)
  no operation moved by 1% of the time
where the time goes in v9:
time: 145 us; the launch traced here: 144 us
  blocking collectives  121 us (83%)
  Pallas kernels  9.29 us (6%)
  starting transfers between devices  7.33 us (5%)
  waiting for transfers between devices  5.46 us (4%)
    all_to_all x7, blocking collectives, gather_parts(): return lax.all_to_all(spread, 'feeder', 0, 0)  76.1 us
    all_to_all x1, blocking collectives, local(): got = lax.all_to_all(sent, 'scen', 0, 0)  28.5 us
    all_to_all x1, blocking collectives, local(): got = lax.all_to_all(back, 'scen', 0, 0)  16.7 us
    pallas_call x12, Pallas kernels, call(): pl.pallas_call(kernel, out_shape=outputs, in_specs=in_specs or [VMEM] * l...  9.29 us
    all_to_all x1, starting transfers between devices, local(): got = lax.all_to_all(spread, 'feeder', 0, 0)  7.33 us
    all_to_all x1, waiting for transfers between devices, local(): got = lax.all_to_all(spread, 'feeder', 0, 0)  5.46 us
  transfers between devices with their start and end apart: 1, of which 1 were waited for; matrix products, arithmetic and copies ran while one was open for 0% of the time, Pallas kernels for 1%

profile of v9, /device:TPU:32, one launch (start us, length us, event | category | flops | bytes accessed | tf_op | source)
XLA Modules:
  0.0 144.3 jit_solution(15976353079245025810)
XLA Ops:
  0.6 1.9 %start_sums.1 = f32[32,3,128]{2,1,0:T(4,128)} custom-call(bf16[384,512]{1,0:T(8,128)(2,1)} %bitcast.13), custom_call_target="tpu_custom_call" | custom-call | tf_op jit(solution)/shard_map/start_sums/pallas_call | solution.py:292
  2.6 7.3 %all-to-all-start = ((f32[32,3,128]{2,1,0:T(4,128)}), f32[32,3,128]{2,1,0:T(4,128)S(1)}, u32[]{:S(2)}, u32[]{:S(2)}) async-start(f32[32,3,128]{2,1,0:T(4,128)} %start_sums.1), calls=%async_computation | async-start | bytes 131072 | tf_op jit(solution)/shard_map/all_to_all | solution.py:336
  9.9 2.1 %prep.1 = (bf16[512,512]{1,0:T(8,128)(2,1)S(1)}, f32[384,512]{1,0:T(8,128)S(1)}, f32[384,512]{1,0:T(8,128)S(1)}, f32[1,512]{1,0:T(1,128)S(1)}, f32[1568,128]{1,0:T(8,128)S(1)}) custom-call(s32[1]{0:T(128)} %bitcast.1.first_ref, f32[16,24]{1,0:T(8,128)} %target_hbm.1, s32[16,24]{1,0:T(8,128)} %bitcast.16, f32[1,16]{1,0:T(1,128)} %bitcast.19, ...), custom_call_target="tpu_custom_call" | custom-call | tf_op jit(solution)/shard_map/prep/pallas_call | solution.py:292
  12.0 5.5 %all-to-all-done.refs_0_ = f32[32,3,128]{2,1,0:T(4,128)S(1)} async-done(((f32[32,3,128]{2,1,0:T(4,128)}), f32[32,3,128]{2,1,0:T(4,128)S(1)}, u32[]{:S(2)}, u32[]{:S(2)}) %all-to-all-start) | async-done | bytes 49184 | tf_op jit(solution)/shard_map/all_to_all | solution.py:336
  17.4 0.5 prox_step.7
  17.9 10.9 %all_to_all.50.refs_0_ = f32[32,3,128]{2,1,0:T(4,128)S(1)} all-to-all(f32[32,3,128]{2,1,0:T(4,128)S(1)} %broadcast_in_dim.21), channel_id=1, replica_groups=mesh['feeder'=32,'scen'=16] {'feeder'}, dimensions={0} | all-to-all | bytes 98304 | tf_op jit(solution)/shard_map/all_to_all | solution.py:313
  28.8 0.5 prox_step.8
  29.3 10.9 %all_to_all.51.refs_0_ = f32[32,3,128]{2,1,0:T(4,128)S(1)} all-to-all(f32[32,3,128]{2,1,0:T(4,128)S(1)} %broadcast_in_dim.22), channel_id=1, replica_groups=mesh['feeder'=32,'scen'=16] {'feeder'}, dimensions={0} | all-to-all | bytes 98304 | tf_op jit(solution)/shard_map/all_to_all | solution.py:313
  40.1 0.5 prox_step.9
  40.6 10.9 %all_to_all.52.refs_0_ = f32[32,3,128]{2,1,0:T(4,128)S(1)} all-to-all(f32[32,3,128]{2,1,0:T(4,128)S(1)} %broadcast_in_dim.23), channel_id=1, replica_groups=mesh['feeder'=32,'scen'=16] {'feeder'}, dimensions={0} | all-to-all | bytes 98304 | tf_op jit(solution)/shard_map/all_to_all | solution.py:313
  51.5 0.5 prox_step.10
  52.0 10.9 %all_to_all.53.refs_0_ = f32[32,3,128]{2,1,0:T(4,128)S(1)} all-to-all(f32[32,3,128]{2,1,0:T(4,128)S(1)} %broadcast_in_dim.24), channel_id=1, replica_groups=mesh['feeder'=32,'scen'=16] {'feeder'}, dimensions={0} | all-to-all | bytes 98304 | tf_op jit(solution)/shard_map/all_to_all | solution.py:313
  62.8 0.5 prox_step.11
  63.3 10.9 %all_to_all.54.refs_0_ = f32[32,3,128]{2,1,0:T(4,128)S(1)} all-to-all(f32[32,3,128]{2,1,0:T(4,128)S(1)} %broadcast_in_dim.25), channel_id=1, replica_groups=mesh['feeder'=32,'scen'=16] {'feeder'}, dimensions={0} | all-to-all | bytes 98304 | tf_op jit(solution)/shard_map/all_to_all | solution.py:313
  74.2 0.5 prox_step.12
  74.7 10.9 %all_to_all.55.refs_0_ = f32[32,3,128]{2,1,0:T(4,128)S(1)} all-to-all(f32[32,3,128]{2,1,0:T(4,128)S(1)} %broadcast_in_dim.26), channel_id=1, replica_groups=mesh['feeder'=32,'scen'=16] {'feeder'}, dimensions={0} | all-to-all | bytes 98304 | tf_op jit(solution)/shard_map/all_to_all | solution.py:313
  85.6 0.5 prox_step.13
  86.0 10.9 %all_to_all.56.refs_0_ = f32[32,3,128]{2,1,0:T(4,128)S(1)} all-to-all(f32[32,3,128]{2,1,0:T(4,128)S(1)} %broadcast_in_dim.27), channel_id=1, replica_groups=mesh['feeder'=32,'scen'=16] {'feeder'}, dimensions={0} | all-to-all | bytes 98304 | tf_op jit(solution)/shard_map/all_to_all | solution.py:313
  96.9 0.0 copy-start
  96.9 0.4 last_step.1
  97.3 28.5 %all_to_all.57.got_ref = f32[16,1,1664]{2,1,0:T(1,128)S(1)} all-to-all(f32[16,1,1664]{2,1,0:T(1,128)S(1)} %get-tuple-element.47), channel_id=1, replica_groups=mesh['feeder'=32,'scen'=16] {'scen'}, dimensions={0} | all-to-all | bytes 212992 | tf_op jit(solution)/shard_map/all_to_all | solution.py:369
  125.8 0.2 owner_chain.1
  126.0 16.7 %all_to_all.58.got_ref = f32[16,3,4,128]{3,2,1,0:T(4,128)S(1)} all-to-all(f32[16,3,4,128]{3,2,1,0:T(4,128)S(1)} %owner_chain.1), channel_id=1, replica_groups=mesh['feeder'=32,'scen'=16] {'scen'}, dimensions={0} | all-to-all | bytes 196608 | tf_op jit(solution)/shard_map/all_to_all | solution.py:372
  142.7 0.0 copy-done
  142.7 1.6 %finish.1 = (f32[384,512]{1,0:T(8,128)}, f32[384,512]{1,0:T(8,128)}, f32[384,512]{1,0:T(8,128)}) custom-call(f32[16,3,4,128]{3,2,1,0:T(4,128)S(1)} %all_to_all.58.got_ref, f32[384,512]{1,0:T(8,128)S(1)} %get-tuple-element.48.own_ref, f32[1568,128]{1,0:T(8,128)S(1)} %get-tuple-element.46.refs_2_.thin_ref, f32[384,512]{1,0:T(8,128)S(1)} %get-tuple-element.49.x_ref, ...), custom_call_target="tpu_custom_call" | custom-call | tf_op jit(solution)/shard_map/finish/pallas_call | solution.py:292
  (7 shorter events, 0.1 us)
Async XLA Ops:
  2.6 14.9 %all-to-all-start = ((f32[32,3,128]{2,1,0:T(4,128)}), f32[32,3,128]{2,1,0:T(4,128)S(1)}, u32[]{:S(2)}, u32[]{:S(2)}) async-start(f32[32,3,128]{2,1,0:T(4,128)} %start_sums.1), calls=%async_computation | async-start | bytes 131072 | tf_op jit(solution)/shard_map/all_to_all | solution.py:336
  96.9 45.8 %copy-start = (f32[16,24,512]{2,1,0:T(8,128)S(1)}, f32[16,24,512]{2,1,0:T(8,128)}, u32[]{:S(2)}) copy-start(f32[16,24,512]{2,1,0:T(8,128)} %param.11) | copy-start | bytes 2359300
